TPU v7x, 32 devices: a whole 2x2x4 slice. The times are simulated.
32 devices in a mesh: row: 8 (over y, x, core), col: 4 (over z).
Axes of the slice: x: 2, y: 2, z: 4, core: 2. Of those that a mesh axis runs over, the one named last changes fastest.
Arguments:
- covariance: float32 [8192, 8192], P('row', 'col'), as said below
- innovations: float32 [512, 8, 1024], P('row', None, 'col'), may hold values from -6 to 6
- block_owner: int32 [32], replicated, may hold values from 0 to 31, as said below
- panel_index: int32 [1], replicated, may hold values from 0 to 15
Outputs:
- factor: float32 [8192, 8192], P('row', 'col')
- solved: float32 [512, 8192], P('col', 'row')
Inputs may be any that keep to these rules, and one draw needn't show every extreme that they name: Storage block s holds global block block_owner[s]; every global block appears once; the storage blocks s with one value of s // 4 hold the blocks of one residue modulo 8, rising with s. `covariance`: symmetric positive definite.
All inputs are finite; a program needn't handle non-finite values.
Results may differ from a plain program's by a relative error of at most 0.0016.
Values may be sent and summed in bfloat16 or wider, within the bound.
A program may use at most 128 MiB of HBM per device.

v0:
```python
import jax
import jax.numpy as jnp
from jax import lax
from jax.sharding import PartitionSpec as P

B = 256
PANELS = 2


CONTRACT_LAST = (((1,), (1,)), ((), ()))


def spread(value, axis, source):
    kept = jnp.where(lax.axis_index(axis) == source, value, 0).astype(value.dtype)
    return lax.psum(kept, axis)


def lower_solve(factor, right_side):
    return jax.scipy.linalg.solve_triangular(factor, right_side, lower=True)


def outer_rows(left, right):
    return lax.dot_general(left, right, CONTRACT_LAST, preferred_element_type=jnp.float32)


def locate(block_owner, target):
    positions = jnp.arange(block_owner.shape[0], dtype=jnp.int32)
    return jnp.sum(jnp.where(block_owner == target, positions, 0))


def per_device(covariance, innovations, block_owner, panel_index):
    panel_width = B
    local_rows, local_cols = covariance.shape
    row_blocks = local_rows // panel_width
    column_blocks = local_cols // panel_width
    row_here = lax.axis_index("row")
    column_here = lax.axis_index("col")
    relaid = lax.all_to_all(
        lax.all_to_all(innovations, "row", split_axis=1, concat_axis=0, tiled=True),
        "col",
        split_axis=0,
        concat_axis=2,
        tiled=True,
    )
    solved = relaid.reshape(relaid.shape[0], local_rows)
    owner_rows = jnp.repeat(
        lax.dynamic_slice_in_dim(block_owner, row_here * row_blocks, row_blocks), panel_width
    )
    owner_columns = jnp.repeat(
        lax.dynamic_slice_in_dim(block_owner, column_here * column_blocks, column_blocks),
        panel_width,
    )
    matrix = covariance
    ahead_column = None
    for panel_turn in range(PANELS):
        target = panel_index[0] + panel_turn
        slot_index = locate(block_owner, target)
        row_root = slot_index // row_blocks
        column_root = slot_index // column_blocks
        row_start = slot_index % row_blocks * panel_width
        column_start = slot_index % column_blocks * panel_width
        column_local = lax.dynamic_slice_in_dim(matrix, column_start, panel_width, 1)
        ahead_column = None
        live_rows = owner_rows > target
        live_columns = owner_columns > target
        column = spread(column_local, "col", column_root)
        diagonal_local = lax.dynamic_slice_in_dim(column, row_start, panel_width, 0)
        innovation_local = lax.dynamic_slice_in_dim(solved, row_start, panel_width, 1)
        diagonal, innovation_block = (
            spread(diagonal_local, "row", row_root),
            spread(innovation_local, "row", row_root),
        )
        factor = jnp.linalg.cholesky(diagonal)
        panel_rows = jnp.where(live_rows[:, None], lower_solve(factor, column.T).T, 0.0)
        rows_half = panel_rows.astype(jnp.bfloat16)
        row_local = lax.dynamic_slice_in_dim(matrix, row_start, panel_width, 0)
        row_panel = spread(row_local, "row", row_root)
        panel_columns = jnp.where(live_columns[:, None], lower_solve(factor, row_panel).T, 0.0)
        columns_half = panel_columns.astype(jnp.bfloat16)
        matrix = matrix - outer_rows(rows_half, columns_half)
        whitened = lower_solve(factor, innovation_block.T).T
        solved = solved - outer_rows(whitened.astype(jnp.bfloat16), rows_half)
        spot_old = lax.dynamic_slice_in_dim(solved, row_start, panel_width, 1)
        spot_new = jnp.where(row_here == row_root, whitened, spot_old)
        solved = lax.dynamic_update_slice_in_dim(solved, spot_new, row_start, 1)
        row_old = lax.dynamic_slice_in_dim(matrix, row_start, panel_width, 0)
        row_new = jnp.where((row_here == row_root) & live_columns[None, :], 0.0, row_old)
        matrix = lax.dynamic_update_slice_in_dim(matrix, row_new, row_start, 0)
        column_old = lax.dynamic_slice_in_dim(matrix, column_start, panel_width, 1)
        column_new = jnp.where(live_rows[:, None], panel_rows, column_old)
        diagonal_spot = lax.dynamic_update_slice_in_dim(column_new, factor, row_start, 0)
        column_new = jnp.where(row_here == row_root, diagonal_spot, column_new)
        column_new = jnp.where(column_here == column_root, column_new, column_old)
        matrix = lax.dynamic_update_slice_in_dim(matrix, column_new, column_start, 1)
    return (matrix, solved)


def solution(mesh):
    placed = (P("row", "col"), P("row", None, "col"), P(), P())
    return jax.shard_map(
        per_device,
        mesh=mesh,
        in_specs=placed,
        out_specs=(P("row", "col"), P("col", "row")),
        check_vma=False,
    )
```

profile of v0, /device:TPU:0, one launch (start us, length us, event | category | flops | bytes accessed | tf_op | source)
XLA Modules:
  0.0 469.2 jit_solution(13405228891102686264)
XLA Ops:
  7.2 2.0 copy.81
  9.2 5.2 %all-to-all-start = ((f32[64,8,256]{2,0,1:T(8,128)}), f32[64,8,256]{2,0,1:T(8,128)S(1)}, u32[]{:S(2)}, u32[]{:S(2)}) async-start(f32[64,8,256]{2,0,1:T(8,128)} %copy.81), calls=%async_computation | async-start | bytes 1048576 | tf_op jit(solution)/shard_map/all_to_all | solution.py:39
  15.1 0.6 fusion.56
  18.3 9.3 %copy.69 = f32[1024,2048]{0,1:T(8,128)} copy(f32[1024,2048]{1,0:T(8,128)} %param.11) | data formatting | bytes 16777216 | tf_op args[0]
  27.6 2.3 dynamic-slice_select_fusion.3
  30.0 1.3 copy.82
  31.3 4.9 %all-to-all-start.1 = ((f32[512,1,256]{2,1,0:T(1,128)}), f32[512,1,256]{2,1,0:T(1,128)S(1)}, u32[]{:S(2)}, u32[]{:S(2)}) async-start(f32[512,1,256]{2,1,0:T(1,128)} %copy.82), calls=%async_computation.1 | async-start | bytes 1048576 | tf_op jit(solution)/shard_map/all_to_all | solution.py:38
  36.2 3.2 dynamic-slice_select_fusion.1
  39.4 55.2 %all-reduce.8.cloned.1.call-done = f32[1024,256]{0,1:T(8,128)} async-done(((f32[1024,256]{0,1:T(8,128)}), f32[1024,256]{0,1:T(8,128)}) %all-reduce.8.cloned.1.call-update) | async-done | bytes 1048592 | tf_op jit(solution)/shard_map/psum | solution.py:15
  94.5 1.7 dynamic-slice_select_fusion.7
  96.4 0.7 select_bitcast_fusion.1
  100.4 61.4 %all-reduce.14.cloned.1.call-done = (f32[256,2048]{0,1:T(8,128)}, f32[256,256]{0,1:T(8,128)}, f32[256,128]{1,0:T(8,128)}) async-done(((f32[256,2048]{0,1:T(8,128)}, f32[256,256]{0,1:T(8,128)}, f32[256,128]{1,0:T(8,128)}), (f32[256,2048]{0,1:T(8,128)}, f32[256,256]{0,1:T(8,128)}, f32[256,128]{1,0:T(8,128)})) %all-reduce.14.cloned.1.call-update) | async-done | bytes 2490384 | tf_op jit(solution)/shard_map/psum | solution.py:15
  161.8 1.1 copy.59
  162.9 1.0 fusion.21
  163.9 11.7 %cholesky.130 = f32[128,128]{1,0:T(8,128)S(1)} custom-call(f32[128,128]{1,0:T(8,128)S(1)} %cholesky.194), custom_call_target="Cholesky" | custom-call | tf_op jit(solution)/shard_map/jit(cholesky)/cholesky | solution.py:73
  175.6 9.8 %custom-call.21 = f32[1,128,128]{1,2,0:T(8,128)S(1)} custom-call(f32[1,128,128]{2,1,0:T(8,128)S(1)} %get-tuple-element.163), custom_call_target="InvertDiagBlocksLowerTriangular" | custom-call | tf_op jit(solution)/shard_map/jit(cholesky)/cholesky | solution.py:73
  185.9 11.7 %cholesky.147 = f32[128,128]{1,0:T(8,128)S(1)} custom-call(f32[128,128]{1,0:T(8,128)S(1)} %convolution_subtract_fusion.11), custom_call_target="Cholesky" | custom-call | tf_op jit(solution)/shard_map/jit(cholesky)/cholesky | solution.py:73
  198.0 0.7 compare_reduce_fusion.2
  200.1 4.3 while.12
  200.2 0.6 fusion.85
  200.8 1.3 dynamic-slice.26
  202.3 0.6 fusion.85
  202.9 1.3 dynamic-slice.26
  204.3 19.7 %custom-call.22 = f32[2,128,128]{1,2,0:T(8,128)S(1)} custom-call(f32[2,128,128]{2,1,0:T(8,128)S(1)} %get-tuple-element.48), custom_call_target="InvertDiagBlocksLowerTriangular" | custom-call | tf_op jit(solution)/shard_map/jit(_solve_triangular)/triangular_solve | solution.py:19
  224.0 2.3 fusion.6
  226.3 3.1 convolution_subtract_fusion.3
  229.4 1.0 copy.67
  230.7 1.7 fusion.18
  232.4 1.7 convolution_subtract_fusion.7
  234.1 0.6 fusion.41
  234.7 1.0 fusion.40
  235.7 4.3 convolution_subtract_fusion.1
  241.1 3.4 copy-done
  244.5 1.1 dynamic-slice_select_fusion.2
  246.8 0.7 select_bitcast_fusion
  247.5 3.0 dynamic-slice_select_fusion
  250.5 46.5 %all-reduce.10.cloned.1.call-done = f32[1024,256]{0,1:T(8,128)} async-done(((f32[1024,256]{0,1:T(8,128)}), f32[1024,256]{0,1:T(8,128)}) %all-reduce.10.cloned.1.call-update) | async-done | bytes 1048592 | tf_op jit(solution)/shard_map/psum | solution.py:15
  297.0 1.7 dynamic-slice_select_fusion.6
  298.9 65.3 %all-reduce.12.cloned.1.call-done = (f32[256,2048]{0,1:T(8,128)}, f32[256,256]{0,1:T(8,128)}, f32[256,128]{1,0:T(8,128)}) async-done(((f32[256,2048]{0,1:T(8,128)}, f32[256,256]{0,1:T(8,128)}, f32[256,128]{1,0:T(8,128)}), (f32[256,2048]{0,1:T(8,128)}, f32[256,256]{0,1:T(8,128)}, f32[256,128]{1,0:T(8,128)})) %all-reduce.12.cloned.1.call-update) | async-done | bytes 2490384 | tf_op jit(solution)/shard_map/psum | solution.py:15
  364.2 1.1 copy.71
  365.3 1.0 fusion.20
  366.3 11.7 %cholesky.164 = f32[128,128]{1,0:T(8,128)S(1)} custom-call(f32[128,128]{1,0:T(8,128)S(1)} %cholesky.197), custom_call_target="Cholesky" | custom-call | tf_op jit(solution)/shard_map/jit(cholesky)/cholesky | solution.py:73
  378.1 9.8 %custom-call.24 = f32[1,128,128]{1,2,0:T(8,128)S(1)} custom-call(f32[1,128,128]{2,1,0:T(8,128)S(1)} %get-tuple-element.161), custom_call_target="InvertDiagBlocksLowerTriangular" | custom-call | tf_op jit(solution)/shard_map/jit(cholesky)/cholesky | solution.py:73
  388.4 11.7 %cholesky.181 = f32[128,128]{1,0:T(8,128)S(1)} custom-call(f32[128,128]{1,0:T(8,128)S(1)} %convolution_subtract_fusion.10), custom_call_target="Cholesky" | custom-call | tf_op jit(solution)/shard_map/jit(cholesky)/cholesky | solution.py:73
  400.4 0.7 compare_reduce_fusion
  401.1 0.6 compare_reduce_fusion.1
  403.1 4.5 while.13
  404.0 1.4 dynamic-slice.28
  405.5 0.6 fusion.86
  406.1 1.4 dynamic-slice.28
  407.6 19.7 %custom-call.25 = f32[2,128,128]{1,2,0:T(8,128)S(1)} custom-call(f32[2,128,128]{2,1,0:T(8,128)S(1)} %get-tuple-element.50), custom_call_target="InvertDiagBlocksLowerTriangular" | custom-call | tf_op jit(solution)/shard_map/jit(_solve_triangular)/triangular_solve | solution.py:19
  427.3 2.3 fusion.4
  429.6 3.1 convolution_subtract_fusion.2
  432.6 1.0 copy.78
  434.5 1.7 fusion.16
  436.2 0.6 convolution_subtract_fusion.6
  436.8 0.6 fusion.44
  437.9 1.0 copy.89
  438.9 1.0 fusion.43
  439.9 6.2 %convolution_subtract_fusion = f32[1024,2048]{0,1:T(8,128)} fusion(f32[1024,2048]{0,1:T(8,128)} %copy-done, bf16[128,2048]{0,1:T(8,128)(2,1)S(1)} %fusion.43, bf16[128,2048]{0,1:T(8,128)(2,1)S(1)} %copy-done.1, pred[2048]{0:T(1024)(128)(4,1)S(1)} %gt.75, f32[128,1024]{1,0:T(8,128)S(1)} %fusion.44, f32[128,1024]{1,0:T(8,128)S(1)} %fusion.16, ...), kind=kOutput, calls=%fused_computation.4 | convolution fusion | flops 1079771136 | bytes 18877440 | tf_op jit(solution)/shard_map/dot_general | solution.py:23
  446.1 3.4 select_dynamic-update-slice_fusion
  449.4 1.4 dynamic-slice_select_fusion.4
  450.9 2.4 select_dynamic-update-slice_fusion.2
  453.3 9.1 %copy.88 = f32[1024,2048]{1,0:T(8,128)} copy(f32[1024,2048]{0,1:T(8,128)} %select_dynamic-update-slice_fusion.2) | data formatting | bytes 16777216
  (93 shorter events, 8.2 us)
Async XLA Ops:
  7.2 7.9 %copy-start.6 = (s32[32]{0:T(128)S(1)}, s32[32]{0:T(128)}, u32[]{:S(2)}) copy-start(s32[32]{0:T(128)} %param.13) | copy-start | bytes 388
  9.2 20.8 %all-to-all-start = ((f32[64,8,256]{2,0,1:T(8,128)}), f32[64,8,256]{2,0,1:T(8,128)S(1)}, u32[]{:S(2)}, u32[]{:S(2)}) async-start(f32[64,8,256]{2,0,1:T(8,128)} %copy.81), calls=%async_computation | async-start | bytes 1048576 | tf_op jit(solution)/shard_map/all_to_all | solution.py:39
  14.4 80.1 %all-reduce.8.cloned.1.call-start = ((), (), s32[]{:S(2)}) async-start(), calls=%async_computation.2 | async-start | bytes 2097152 | tf_op jit(solution)/shard_map/psum | solution.py:15
  31.3 64.9 %all-to-all-start.1 = ((f32[512,1,256]{2,1,0:T(1,128)}), f32[512,1,256]{2,1,0:T(1,128)S(1)}, u32[]{:S(2)}, u32[]{:S(2)}) async-start(f32[512,1,256]{2,1,0:T(1,128)} %copy.82), calls=%async_computation.1 | async-start | bytes 1048576 | tf_op jit(solution)/shard_map/all_to_all | solution.py:38
  36.2 125.6 %all-reduce.14.cloned.1.call-start = ((), (), s32[]{:S(2)}) async-start(), calls=%async_computation.5 | async-start | bytes 4980736 | tf_op jit(solution)/shard_map/psum | solution.py:15
  97.1 199.9 %all-reduce.10.cloned.1.call-start = ((), (), s32[]{:S(2)}) async-start(), calls=%async_computation.3 | async-start | bytes 2097152 | tf_op jit(solution)/shard_map/psum | solution.py:15
  226.3 4.1 copy-start.4
  232.3 3.4 copy-start.2
  241.1 3.4 copy-start
  245.6 118.6 %all-reduce.12.cloned.1.call-start = ((), (), s32[]{:S(2)}) async-start(), calls=%async_computation.4 | async-start | bytes 4980736 | tf_op jit(solution)/shard_map/psum | solution.py:15
  429.6 4.1 copy-start.5
  433.6 2.6 copy-start.3
  437.8 2.0 copy-start.1
Sparse Core Ops, SparseCore 0:
  30.1 64.3 all-reduce.7
  98.6 63.1 all-reduce.13
  245.7 51.2 all-reduce.9
  301.0 63.1 all-reduce.11
where the time goes:
time: 473 us; the launch traced here: 469 us
  waiting for transfers between devices  228 us (48%)
  other arithmetic  133 us (28%)
  local copies, waits for them, and re-layouts  39.7 us (8%)
  matrix products  33.4 us (7%)
  between operations  22.8 us (5%)
  starting transfers between devices  10.9 us (2%)
    psum x4, waiting for transfers between devices, spread(): return lax.psum(kept, axis)  228 us
    another operation x13, other arithmetic, per_device(): factor = jnp.linalg.cholesky(diagonal)  68.6 us
    another operation x5, other arithmetic, lower_solve(): return jax.scipy.linalg.solve_triangular(factor, right_side, lower=True)  39.4 us
    unnamed x19, local copies, waits for them, and re-layouts  24.8 us
    another operation x18, matrix products, lower_solve(): return jax.scipy.linalg.solve_triangular(factor, right_side, lower=True)  21.3 us
    select_n x6, other arithmetic, spread(): jnp.where(lax.axis_index(axis) == source, value, 0).astype(value.dtype)  13 us
    dot_general x4, matrix products, outer_rows(): lax.dot_general(left, right, CONTRACT_LAST, preferred_element_type=jnp.fl...  11.2 us
    another operation x25, local copies, waits for them, and re-layouts, lower_solve(): return jax.scipy.linalg.solve_triangular(factor, right_side, lower=True)  10.2 us
  transfers between devices with their start and end apart: 6, of which 4 were waited for; matrix products, arithmetic and copies ran while one was open for 5% of the time, Pallas kernels for 0%

commit v1 on v0

v1 whole, which is shorter than its diff:
```python
import functools

import jax
import jax.numpy as jnp
from jax import lax
from jax.experimental import pallas as pl
from jax.experimental.pallas import tpu as pltpu
from jax.sharding import PartitionSpec as P

B = 256
PANELS = 2
SUB = 64
G8 = SUB // 8
LANES = 128
TW = 2 * B // LANES
HIGHEST = lax.Precision.HIGHEST

LAST = (((1,), (1,)), ((), ()))
FIRST = (((0,), (0,)), ((), ()))
PLAIN = (((1,), (0,)), ((), ()))


def dot(a, b, dims=PLAIN, precision=None):
    return lax.dot_general(a, b, dims, precision=precision, preferred_element_type=jnp.float32)


def split_bf16(x):
    hi = x.astype(jnp.bfloat16)
    lo = (x - hi.astype(jnp.float32)).astype(jnp.bfloat16)
    return hi, lo


def dot3(a, b, dims=PLAIN):
    ah, al = split_bf16(a)
    bh, bl = split_bf16(b)
    return dot(ah, bh, dims) + (dot(ah, bl, dims) + dot(al, bh, dims))


def lanes(x):
    return jnp.broadcast_to(x, (8, LANES))


def factor_panel(s_ref, p_ref):
    sub_iota = lax.broadcasted_iota(jnp.int32, (8, LANES), 0)
    rows = [[s_ref[8 * g : 8 * g + 8, LANES * t : LANES * (t + 1)] for t in range(TW)] for g in range(G8)]
    for b in range(G8):
        c0 = 8 * b
        col = [[lanes(rows[g][0][:, c0 + j : c0 + j + 1]) for j in range(8)] for g in range(b, G8)]
        e = [[lanes(col[0][j][i : i + 1, :]) for j in range(i + 1)] for i in range(8)]
        r = []
        l = [[None] * 8 for _ in range(8)]
        for j in range(8):
            rj = lax.rsqrt(e[j][j])
            r.append(rj)
            for i in range(j + 1, 8):
                l[i][j] = e[i][j] * rj
            for i in range(j + 1, 8):
                for k in range(j + 1, i + 1):
                    e[i][k] = e[i][k] - l[i][j] * l[k][j]
        y = []
        for i in range(8):
            yi = []
            for t in range(TW):
                v = lanes(rows[b][t][i : i + 1, :])
                for j in range(i):
                    v = v - l[i][j] * y[j][t]
                yi.append(v * r[i])
            y.append(yi)
        for t in range(TW):
            u = y[0][t]
            for i in range(1, 8):
                u = jnp.where(sub_iota == i, y[i][t], u)
            p_ref[8 * b : 8 * b + 8, LANES * t : LANES * (t + 1)] = u
        for g in range(b + 1, G8):
            cs = []
            for j in range(8):
                v = col[g - b][j]
                for k in range(j):
                    v = v - l[j][k] * cs[k]
                cs.append(v * r[j])
            for t in range(TW):
                v = rows[g][t]
                for j in range(8):
                    v = v - cs[j] * y[j][t]
                rows[g][t] = v


def factor_kernel(d_ref, u_ref, z_ref, x_ref, a_ref, s_ref, p_ref):
    row_i = lax.broadcasted_iota(jnp.int32, (B, B), 0)
    col_i = lax.broadcasted_iota(jnp.int32, (B, B), 1)
    a_ref[...] = d_ref[0]

    def panel(turn, carry):
        s_ref[:, :B] = a_ref[...]
        s_ref[:, B:] = jnp.where(row_i == col_i, 1.0, 0.0)

        def step(k, carry):
            factor_panel(s_ref, p_ref)
            start = pl.multiple_of(k * SUB, SUB)
            u_ref[turn, pl.ds(start, SUB), :] = pltpu.roll(p_ref[:, :B], start, 1)
            z_ref[turn, pl.ds(start, SUB), :] = p_ref[:, B:]
            left = p_ref[:, :B]
            rolled = pltpu.roll(left, B - SUB, 1)
            lane = lax.broadcasted_iota(jnp.int32, (SUB, B), 1)
            rolled = jnp.where(lane < B - SUB, rolled, 0.0)
            upd_a = dot(rolled, rolled, FIRST, HIGHEST)
            upd_z = dot(rolled, p_ref[:, B:], FIRST, HIGHEST)
            keep = B - SUB
            old = pltpu.roll(s_ref[SUB:, :B], B - SUB, 1)
            lane2 = lax.broadcasted_iota(jnp.int32, (keep, B), 1)
            old = jnp.where(lane2 < keep, old, 0.0)
            old_z = s_ref[SUB:, B:]
            s_ref[:keep, :B] = old - upd_a[:keep]
            s_ref[:keep, B:] = old_z - upd_z[:keep]
            s_ref[keep:, :] = jnp.zeros((SUB, 2 * B), jnp.float32)
            return carry

        lax.fori_loop(0, B // SUB, step, 0)

        @pl.when(turn == 0)
        def _():
            zt = jnp.where(row_i >= col_i, z_ref[0], 0.0)
            low = dot3(d_ref[1], zt, LAST)
            half = low.astype(jnp.bfloat16)
            x_ref[...] = half
            a_ref[...] = d_ref[2] - dot(half, half, LAST)

        return carry

    lax.fori_loop(0, PANELS, panel, 0)


def factor_pair(blocks):
    return pl.pallas_call(
        factor_kernel,
        out_shape=(
            jax.ShapeDtypeStruct((PANELS, B, B), jnp.float32),
            jax.ShapeDtypeStruct((PANELS, B, B), jnp.float32),
            jax.ShapeDtypeStruct((B, B), jnp.bfloat16),
        ),
        scratch_shapes=[
            pltpu.VMEM((B, B), jnp.float32),
            pltpu.VMEM((B, 2 * B), jnp.float32),
            pltpu.VMEM((SUB, 2 * B), jnp.float32),
        ],
        cost_estimate=pl.CostEstimate(flops=100_000_000, bytes_accessed=2_000_000, transcendentals=0),
    )(blocks)


def panel_kernel(owner_ref, at_ref, cols_ref, z_ref, x_ref, out_ref, half_ref, *, blocks):
    i = pl.program_id(0)
    own = owner_ref[i]
    g = at_ref[0]
    p0 = dot3(cols_ref[:, :B], z_ref[0], LAST)
    p0 = jnp.where(own > g, p0, 0.0)
    h0 = p0.astype(jnp.bfloat16)
    c1 = cols_ref[:, B:] - dot(h0, x_ref[...], LAST)
    p1 = dot3(c1, z_ref[1], LAST)
    p1 = jnp.where(own > g + 1, p1, 0.0)
    out_ref[:, :B] = p0
    out_ref[:, B:] = p1
    half_ref[:, :B] = h0
    half_ref[:, B:] = p1.astype(jnp.bfloat16)


def solve_rows(owner, at, cols, z, x):
    rows = cols.shape[0]
    return pl.pallas_call(
        functools.partial(panel_kernel, blocks=rows // B),
        grid_spec=pltpu.PrefetchScalarGridSpec(
            num_scalar_prefetch=2,
            grid=(rows // B,),
            in_specs=[
                pl.BlockSpec((B, 2 * B), lambda i, o, a: (i, 0)),
                pl.BlockSpec((PANELS, B, B), lambda i, o, a: (0, 0, 0)),
                pl.BlockSpec((B, B), lambda i, o, a: (0, 0)),
            ],
            out_specs=[
                pl.BlockSpec((B, 2 * B), lambda i, o, a: (i, 0)),
                pl.BlockSpec((B, 2 * B), lambda i, o, a: (i, 0)),
            ],
        ),
        out_shape=(
            jax.ShapeDtypeStruct((rows, 2 * B), jnp.float32),
            jax.ShapeDtypeStruct((rows, 2 * B), jnp.bfloat16),
        ),
    )(owner, at, cols, z, x)


def update_kernel(ro_ref, co_ref, at_ref, w_ref, r_ref, z_ref, x_ref, half_ref, full_ref, f_ref, o_ref, *, rb):
    j = pl.program_id(0)
    g = at_ref[0]
    cown = co_ref[j]
    q0 = dot3(z_ref[0], r_ref[:B].astype(jnp.float32))
    q0 = jnp.where(cown > g, q0, 0.0).astype(jnp.bfloat16)
    r1 = r_ref[B:].astype(jnp.float32) - dot(x_ref[...], q0)
    q1 = dot3(z_ref[1], r1)
    q1 = jnp.where(cown > g + 1, q1, 0.0).astype(jnp.bfloat16)
    for i in range(rb):
        span = slice(i * B, (i + 1) * B)
        rown = ro_ref[i]
        new = w_ref[span] - (dot(half_ref[span, :B], q0) + dot(half_ref[span, B:], q1))
        dead = ((rown == g) & (cown > g)) | ((rown == g + 1) & (cown > g + 1))
        o_ref[span] = jnp.where(dead, 0.0, new)

        @pl.when((cown == g) & (rown > g))
        def _():
            o_ref[span] = full_ref[span, :B]

        @pl.when((cown == g) & (rown == g))
        def _():
            o_ref[span] = f_ref[0]

        @pl.when((cown == g + 1) & (rown > g + 1))
        def _():
            o_ref[span] = full_ref[span, B:]

        @pl.when((cown == g + 1) & (rown == g + 1))
        def _():
            o_ref[span] = f_ref[1]


def update(ro, co, at, w, rowpanel, z, x, half, full, factors):
    rows, cols = w.shape
    fixed2 = lambda j, a, b, c: (0, 0)
    fixed3 = lambda j, a, b, c: (0, 0, 0)
    stripe = lambda j, a, b, c: (0, j)
    return pl.pallas_call(
        functools.partial(update_kernel, rb=rows // B),
        grid_spec=pltpu.PrefetchScalarGridSpec(
            num_scalar_prefetch=3,
            grid=(cols // B,),
            in_specs=[
                pl.BlockSpec((rows, B), stripe),
                pl.BlockSpec((2 * B, B), stripe),
                pl.BlockSpec((PANELS, B, B), fixed3),
                pl.BlockSpec((B, B), fixed2),
                pl.BlockSpec((rows, 2 * B), fixed2),
                pl.BlockSpec((rows, 2 * B), fixed2),
                pl.BlockSpec((PANELS, B, B), fixed3),
            ],
            out_specs=pl.BlockSpec((rows, B), stripe),
        ),
        out_shape=jax.ShapeDtypeStruct((rows, cols), jnp.float32),
    )(ro, co, at, w, rowpanel, z, x, half, full, factors)


def locate(block_owner, target):
    positions = jnp.arange(block_owner.shape[0], dtype=jnp.int32)
    return jnp.sum(jnp.where(block_owner == target, positions, 0))


def per_device(covariance, innovations, block_owner, panel_index):
    local_rows, local_cols = covariance.shape
    row_blocks = local_rows // B
    column_blocks = local_cols // B
    r_here = lax.axis_index("row")
    c_here = lax.axis_index("col")
    g = panel_index[0]
    slots = [locate(block_owner, g + t) for t in range(PANELS)]
    rroot = [s // row_blocks for s in slots]
    croot = [s // column_blocks for s in slots]
    rstart = [s % row_blocks * B for s in slots]
    cstart = [s % column_blocks * B for s in slots]

    def block(t, u):
        tile = lax.dynamic_slice(covariance, (rstart[t], cstart[u]), (B, B))
        return jnp.where((r_here == rroot[t]) & (c_here == croot[u]), tile, 0.0)

    blocks = lax.psum(jnp.stack([block(0, 0), block(1, 0), block(1, 1)]), ("row", "col"))
    cols = jnp.concatenate(
        [
            jnp.where(c_here == croot[t], lax.dynamic_slice_in_dim(covariance, cstart[t], B, 1), 0.0)
            for t in range(PANELS)
        ],
        axis=1,
    )
    cols = lax.psum(cols, "col")
    rowpanel = jnp.concatenate(
        [
            jnp.where(r_here == rroot[t], lax.dynamic_slice_in_dim(covariance, rstart[t], B, 0), 0.0)
            for t in range(PANELS)
        ],
        axis=0,
    )
    rowpanel = lax.psum(rowpanel.astype(jnp.bfloat16), "row")

    relaid = lax.all_to_all(
        lax.all_to_all(innovations, "row", split_axis=1, concat_axis=0, tiled=True),
        "col",
        split_axis=0,
        concat_axis=2,
        tiled=True,
    )
    v = relaid.reshape(relaid.shape[0], local_rows)
    vs = jnp.concatenate(
        [
            jnp.where(r_here == rroot[t], lax.dynamic_slice_in_dim(v, rstart[t], B, 1), 0.0)
            for t in range(PANELS)
        ],
        axis=1,
    )
    vs = lax.psum(vs, "row")

    upper, z, x = factor_pair(blocks)
    tri = jnp.tril(jnp.ones((B, B), jnp.bool_))
    factors = jnp.where(tri, upper.transpose(0, 2, 1), 0.0)
    z = jnp.where(tri, z, 0.0)
    at = panel_index
    ro = lax.dynamic_slice_in_dim(block_owner, r_here * row_blocks, row_blocks)
    co = lax.dynamic_slice_in_dim(block_owner, c_here * column_blocks, column_blocks)
    full, half = solve_rows(ro, at, cols, z, x)
    w0 = dot3(vs[:, :B], z[0], LAST)
    w0h = w0.astype(jnp.bfloat16)
    w1 = dot3(vs[:, B:] - dot(w0h, x, LAST), z[1], LAST)
    w1h = w1.astype(jnp.bfloat16)
    owner_lane = jnp.repeat(ro, B)[None, :]
    wide0 = jnp.tile(w0, (1, row_blocks))
    wide1 = jnp.tile(w1, (1, row_blocks))
    v = v - dot(jnp.concatenate([w0h, w1h], axis=1), half, LAST)
    v = jnp.where(owner_lane == g, wide0, v)
    v = jnp.where(owner_lane == g + 1, wide1, v)
    matrix = update(ro, co, at, covariance, rowpanel, z, x, half, full, factors)
    return (matrix, v)


def solution(mesh):
    placed = (P("row", "col"), P("row", None, "col"), P(), P())
    return jax.shard_map(
        per_device,
        mesh=mesh,
        in_specs=placed,
        out_specs=(P("row", "col"), P("col", "row")),
        check_vma=False,
    )
```

time: 473 us -> 404 us (0.85)
  other arithmetic: 133 us -> 13.6 us
  waiting for transfers between devices: 228 us -> 287 us
  Pallas kernels: 0 us -> 50.2 us
  local copies, waits for them, and re-layouts: 39.7 us -> 5.49 us
  matrix products: 33.4 us -> 7.49 us
  blocking collectives: 0 us -> 14.7 us
  starting transfers between devices: 10.9 us -> 5 us
    another operation x18 -> x3, other arithmetic: 108 us -> 5.04 us  [the longest x13 68.6 us: per_device(): factor = jnp.linalg.cholesky(diagonal)]
    psum x4, waiting for transfers between devices: 228 us -> 284 us  [the longest x1 116 us: per_device(): lax.psum(jnp.stack([block(0, 0), block(1, 0), block(1, 1)]), ('row', 'col'))]
    pallas_call x0 -> x3, Pallas kernels: none -> 50.2 us  [the longest x1 23.1 us: factor_pair(): pl.pallas_call(factor_kernel, out_shape=(jax.ShapeDtypeStruct((PANELS, B,...]
    unnamed x19 -> x13, local copies, waits for them, and re-layouts: 24.8 us -> 1.56 us
    another operation x22 -> x0, matrix products: 22.2 us -> none  [the longest x18 21.3 us: lower_solve(): return jax.scipy.linalg.solve_triangular(factor, right_side, lower=True)]
    all_to_all x0 -> x1, blocking collectives: none -> 14.7 us  [per_device(): lax.all_to_all(innovations, 'row', split_axis=1, concat_axis=0, tiled=True)]
    select_n x10 -> x3, other arithmetic: 14.7 us -> 3.73 us  [the longest x1 1.98 us: per_device(): factors = jnp.where(tri, upper.transpose(0, 2, 1), 0.0)]
    another operation x39 -> x2, local copies, waits for them, and re-layouts: 10.9 us -> 0.18 us  [the longest x1 0.09 us: per_device(): wide1 = jnp.tile(w1, (1, row_blocks))]
  transfers between devices with their start and end apart: 6 -> 5, of which waited for: 4 -> 5; matrix products, arithmetic and copies ran while one was open for 5% -> 6% of each run, Pallas kernels for 0% -> 7%
where the time goes in v1:
time: 404 us; the launch traced here: 403 us
  waiting for transfers between devices  287 us (71%)
  Pallas kernels  50.2 us (12%)
  between operations  19.8 us (5%)
  blocking collectives  14.7 us (4%)
  other arithmetic  13.6 us (3%)
  matrix products  7.49 us (2%)
  local copies, waits for them, and re-layouts  5.49 us (1%)
  starting transfers between devices  5 us (1%)
    psum x1, waiting for transfers between devices, per_device(): lax.psum(jnp.stack([block(0, 0), block(1, 0), block(1, 1)]), ('row', 'col'))  116 us
    psum x1, waiting for transfers between devices, per_device(): cols = lax.psum(cols, 'col')  82.5 us
    psum x1, waiting for transfers between devices, per_device(): rowpanel = lax.psum(rowpanel.astype(jnp.bfloat16), 'row')  55.6 us
    psum x1, waiting for transfers between devices, per_device(): vs = lax.psum(vs, 'row')  29.7 us
    pallas_call x1, Pallas kernels, factor_pair(): pl.pallas_call(factor_kernel, out_shape=(jax.ShapeDtypeStruct((PANELS, B,...  23.1 us
    pallas_call x1, Pallas kernels, update(): pl.pallas_call(functools.partial(update_kernel, rb=rows // B), grid_spec=...  20.6 us
    all_to_all x1, blocking collectives, per_device(): lax.all_to_all(innovations, 'row', split_axis=1, concat_axis=0, tiled=True)  14.7 us
  transfers between devices with their start and end apart: 5, of which 5 were waited for; matrix products, arithmetic and copies ran while one was open for 6% of the time, Pallas kernels for 7%

profile of v1, /device:TPU:0, one launch (start us, length us, event | category | flops | bytes accessed | tf_op | source)
XLA Modules:
  0.0 403.5 jit_solution(5665274769036401987)
XLA Ops:
  7.2 0.0 copy-start.3
  7.2 1.2 copy.11
  8.4 14.7 %all_to_all.33 = f32[64,8,256]{2,0,1:T(8,128)S(1)} all-to-all(f32[64,8,256]{2,0,1:T(8,128)S(1)} %copy.11), channel_id=1, replica_groups=mesh['row'=8,'col'=4] {'row'}, dimensions={1} | all-to-all | bytes 1048576 | tf_op jit(solution)/shard_map/all_to_all | solution.py:289
  23.1 1.3 copy.12
  24.4 4.9 %all-to-all-start.1 = ((f32[512,1,256]{2,1,0:T(1,128)}), f32[512,1,256]{2,1,0:T(1,128)S(1)}, u32[]{:S(2)}, u32[]{:S(2)}) async-start(f32[512,1,256]{2,1,0:T(1,128)} %copy.12), calls=%async_computation.1 | async-start | bytes 1048576 | tf_op jit(solution)/shard_map/all_to_all | solution.py:288
  29.3 0.0 all-reduce.7.cloned.1.call-start
  30.0 0.0 copy-done.3
  30.0 0.7 fusion.9
  35.9 1.4 select_bitcast_fusion.2
  37.2 0.9 pad_maximum_fusion.2
  38.2 0.0 all-reduce.7.cloned.1.call-update
  38.2 0.0 all-reduce.11.cloned.1.call-start
  38.2 1.7 dynamic-slice_select_fusion.1
  40.0 3.3 all-to-all-done.1
  43.3 0.3 copy.13
  43.6 0.1 copy.15
  43.8 0.8 pad_maximum_fusion.3
  44.5 0.0 all-reduce.11.cloned.1.call-update
  44.5 0.0 all-reduce.9.cloned.1.call-start
  44.6 1.6 pad_maximum_fusion.1
  46.2 0.0 all-reduce.9.cloned.1.call-update
  46.3 0.0 all-reduce.5.cloned.1.call-start
  46.3 2.8 select_convert_fusion.1
  49.1 1.6 pad_maximum_fusion
  50.7 0.0 all-reduce.5.cloned.1.call-update
  50.7 0.1 broadcast_compare_fusion.1
  50.8 0.0 copy-start.2
  50.8 0.7 dynamic_slice.34.co_ref
  51.5 0.1 broadcast_in_dim.68
  51.6 0.1 broadcast_in_dim.65
  51.6 116.2 %all-reduce.7.cloned.1.call-done.d_ref = f32[3,256,256]{2,1,0:T(8,128)} async-done(((f32[3,256,256]{2,1,0:T(8,128)}), f32[3,256,256]{2,1,0:T(8,128)}) %all-reduce.7.cloned.1.call-update) | async-done | bytes 786448 | tf_op jit(solution)/shard_map/psum | solution.py:270
  167.8 23.1 %shard_map.59 = (f32[2,256,256]{2,1,0:T(8,128)}, f32[2,256,256]{2,1,0:T(8,128)}, bf16[256,256]{1,0:T(8,128)(2,1)}) custom-call(f32[3,256,256]{2,1,0:T(8,128)} %all-reduce.7.cloned.1.call-done.d_ref), custom_call_target="tpu_custom_call" | custom-call | flops 100000000 | bytes 2000000 | tf_op jit(solution)/shard_map/pallas_call | solution.py:134
  191.0 1.2 copy.10
  192.2 0.0 copy-start.1
  192.2 2.0 bitcast_select_fusion
  194.2 0.0 copy-start
  194.2 29.7 %all-reduce.11.cloned.1.call-done = f32[128,512]{1,0:T(8,128)} async-done(((f32[128,512]{1,0:T(8,128)}), f32[128,512]{1,0:T(8,128)}) %all-reduce.11.cloned.1.call-update) | async-done | bytes 262160 | tf_op jit(solution)/shard_map/psum | solution.py:303
  223.9 1.1 fusion.4
  225.0 0.0 copy-done.2
  225.0 1.1 convolution_add_fusion.2
  226.1 1.1 fusion.21
  227.2 0.0 copy-done.1
  227.2 1.1 convolution_subtract_fusion.1
  228.3 0.2 fusion.5
  228.5 0.2 convolution_add_fusion
  228.7 0.2 fusion.22
  228.9 0.0 copy-done
  228.9 0.1 tile.8
  229.0 0.1 copy.16
  229.1 0.1 tile.20
  229.2 0.1 copy.17
  229.3 82.5 %all-reduce.9.cloned.1.call-done.cols_ref = f32[1024,512]{1,0:T(8,128)} async-done(((f32[1024,512]{1,0:T(8,128)}), f32[1024,512]{1,0:T(8,128)}) %all-reduce.9.cloned.1.call-update) | async-done | bytes 2097168 | tf_op jit(solution)/shard_map/psum | solution.py:278
  311.8 6.4 %shard_map.60 = (f32[1024,512]{1,0:T(8,128)}, bf16[1024,512]{1,0:T(8,128)(2,1)}) custom-call(s32[4]{0:T(128)} %copy-done.2, s32[1]{0:T(128)} %copy.22.at_ref, f32[1024,512]{1,0:T(8,128)} %all-reduce.9.cloned.1.call-done.cols_ref, f32[2,256,256]{2,1,0:T(8,128)} %copy-done, bf16[256,256]{1,0:T(8,128)(2,1)} %get-tuple-element.8.x_ref), custom_call_target="tpu_custom_call" | custom-call | tf_op jit(solution)/shard_map/pallas_call | solution.py:168
  318.2 2.5 fusion.1
  320.7 55.6 %all-reduce.5.cloned.1.call-done.r_ref = bf16[512,2048]{1,0:T(8,128)(2,1)} async-done(((bf16[512,2048]{1,0:T(8,128)(2,1)}), bf16[512,2048]{1,0:T(8,128)(2,1)}) %all-reduce.5.cloned.1.call-update) | async-done | bytes 2097168 | tf_op jit(solution)/shard_map/psum | solution.py:286
  376.3 20.6 %shard_map.61 = f32[1024,2048]{1,0:T(8,128)} custom-call(s32[4]{0:T(128)} %copy-done.2, s32[8]{0:T(128)} %dynamic_slice.34.co_ref, s32[1]{0:T(128)} %copy.22.at_ref, f32[1024,2048]{1,0:T(8,128)} %w_ref.1, bf16[512,2048]{1,0:T(8,128)(2,1)} %all-reduce.5.cloned.1.call-done.r_ref, f32[2,256,256]{2,1,0:T(8,128)} %copy-done, ...), custom_call_target="tpu_custom_call" | custom-call | tf_op jit(solution)/shard_map/pallas_call | solution.py:228
  (6 shorter events, 0.1 us)
Async XLA Ops:
  7.2 22.8 %copy-start.3 = (s32[32]{0:T(128)S(1)}, s32[32]{0:T(128)}, u32[]{:S(2)}) copy-start(s32[32]{0:T(128)} %param.6) | copy-start | bytes 388
  24.4 18.8 %all-to-all-start.1 = ((f32[512,1,256]{2,1,0:T(1,128)}), f32[512,1,256]{2,1,0:T(1,128)S(1)}, u32[]{:S(2)}, u32[]{:S(2)}) async-start(f32[512,1,256]{2,1,0:T(1,128)} %copy.12), calls=%async_computation.1 | async-start | bytes 1048576 | tf_op jit(solution)/shard_map/all_to_all | solution.py:288
  29.3 138.5 %all-reduce.7.cloned.1.call-start = ((), (), s32[]{:S(2)}) async-start(), calls=%async_computation.3 | async-start | bytes 1572864 | tf_op jit(solution)/shard_map/psum | solution.py:270
  38.2 185.7 %all-reduce.11.cloned.1.call-start = ((), (), s32[]{:S(2)}) async-start(), calls=%async_computation.5 | async-start | bytes 524288 | tf_op jit(solution)/shard_map/psum | solution.py:303
  44.5 267.3 %all-reduce.9.cloned.1.call-start = ((), (), s32[]{:S(2)}) async-start(), calls=%async_computation.4 | async-start | bytes 4194304 | tf_op jit(solution)/shard_map/psum | solution.py:278
  46.3 330.0 %all-reduce.5.cloned.1.call-start = ((), (), s32[]{:S(2)}) async-start(), calls=%async_computation.2 | async-start | bytes 4194304 | tf_op jit(solution)/shard_map/psum | solution.py:286
  50.8 174.2 %copy-start.2 = (s32[4]{0:T(128)}, s32[4]{0:T(128)S(1)}, u32[]{:S(2)}) copy-start(s32[4]{0:T(128)S(1)} %get-tuple-element.15.owner_ref.ro_ref) | copy-start | bytes 52
  192.2 35.0 %copy-start.1 = (bf16[256,256]{1,0:T(8,128)(2,1)S(1)}, bf16[256,256]{1,0:T(8,128)(2,1)}, u32[]{:S(2)}) copy-start(bf16[256,256]{1,0:T(8,128)(2,1)} %get-tuple-element.8.x_ref) | copy-start | bytes 393220
  194.2 34.7 %copy-start = (f32[2,256,256]{2,1,0:T(8,128)}, f32[2,256,256]{2,1,0:T(8,128)S(1)}, u32[]{:S(2)}) copy-start(f32[2,256,256]{2,1,0:T(8,128)S(1)} %get-tuple-element.26.z_ref) | copy-start | bytes 1572868
Sparse Core Ops, SparseCore 0:
  38.3 129.4 all-reduce.6
  170.9 52.9 all-reduce.10
  226.2 85.5 all-reduce.8
  315.5 60.7 all-reduce.4

commit v2 on v1

--- a/solution.py
+++ b/solution.py
@@ -245,6 +245,277 @@
     )(ro, co, at, w, rowpanel, z, x, half, full, factors)
 
 
+MESH = pl.DeviceIdType.MESH
+CHUNKS = 16
+
+
+def remote(src, dst, send, recv, where):
+    return pltpu.make_async_remote_copy(
+        src_ref=src, dst_ref=dst, send_sem=send, recv_sem=recv, device_id=where, device_id_type=MESH
+    )
+
+
+class RowSpread:
+    def __init__(self, axis_size, in_ref, acc_ref, core_ref, hop_ref, send, recv):
+        self.bits = [1 << b for b in range(1, axis_size.bit_length() - 1)]
+        self.in_ref, self.acc, self.core, self.hop = in_ref, acc_ref, core_ref, hop_ref
+        self.send, self.recv = send, recv
+        me = lax.axis_index("row")
+        self.me = me
+        self.odd = lax.rem(me, 2)
+        self.mate = me + 1 - 2 * self.odd
+        self.rows = in_ref.shape[0]
+        self.half = self.rows // 2
+        self.quarter = self.rows // 4
+        self.stages = len(self.bits)
+
+    def mine(self, part=0, size=None):
+        start = self.odd * self.half + part * self.quarter
+        return pl.ds(pl.multiple_of(start, self.quarter), self.half if size is None else size)
+
+    def theirs(self):
+        start = (1 - self.odd) * self.half
+        return pl.ds(pl.multiple_of(start, self.half), self.half)
+
+    def partner(self, bit):
+        digit = lax.rem(self.me // bit, 2)
+        return {"row": self.me + bit - 2 * bit * digit}
+
+    def first(self):
+        return remote(self.in_ref.at[self.theirs()], self.core, self.send.at[0], self.recv.at[0], {"row": self.mate})
+
+    def middle(self, stage, part):
+        bit = self.bits[(stage + part) % self.stages]
+        index = 1 + 2 * stage + part
+        return remote(
+            self.acc.at[self.mine(part, self.quarter)],
+            self.hop.at[stage, part],
+            self.send.at[index],
+            self.recv.at[index],
+            self.partner(bit),
+        )
+
+    def final(self):
+        index = 1 + 2 * self.stages
+        rows = self.acc.at[self.mine()]
+        return remote(rows, rows, self.send.at[index], self.recv.at[index], {"row": self.mate})
+
+    def start(self):
+        self.first().start()
+
+    def advance(self, turn):
+        if turn == 0:
+            self.first().wait()
+            self.acc[self.mine()] = self.in_ref[self.mine()] + self.core[...]
+        else:
+            for part in range(2):
+                self.middle(turn - 1, part).wait()
+                rows = self.mine(part, self.quarter)
+                self.acc[rows] = self.acc[rows] + self.hop[turn - 1, part]
+        if turn < self.stages:
+            for part in range(2):
+                self.middle(turn, part).start()
+        else:
+            self.final().start()
+
+    def finish(self):
+        self.final().wait()
+
+
+def spread_scratch(axis_size, shape, dtype):
+    stages = axis_size.bit_length() - 2
+    rows, width = shape
+    count = 2 + 2 * stages
+    return [
+        pltpu.VMEM((rows // 2, width), dtype),
+        pltpu.VMEM((stages, 2, rows // 4, width), dtype),
+        pltpu.SemaphoreType.DMA((count,)),
+        pltpu.SemaphoreType.DMA((count,)),
+    ]
+
+
+def gather_kernel(
+    nr, nc, own, rowp, inn, out, rowout, v,
+    rin, lin, rtx, ltx, rs, rr, ls, lr,
+    core, hop, rowsend, rowrecv, vsend, vrecv, vself,
+):
+    r = lax.axis_index("row")
+    c = lax.axis_index("col")
+    size = own.shape[0] // CHUNKS
+    ratio = nr // nc
+    spread = RowSpread(nr, rowp, rowout, core, hop, rowsend, rowrecv)
+    part_p, width = inn.shape[1], inn.shape[2]
+
+    def chunk(q):
+        return pl.ds(pl.multiple_of(q * size, size), size)
+
+    def right(src, q):
+        return remote(src.at[chunk(q)], rin.at[chunk(q)], rs.at[q], rr.at[q], {"col": c + 1})
+
+    def left(src, q):
+        return remote(src.at[chunk(q)], lin.at[chunk(q)], ls.at[q], lr.at[q], {"col": c - 1})
+
+    spread.start()
+
+    @pl.when(c == 0)
+    def _():
+        lax.fori_loop(0, CHUNKS, lambda q, k: (right(own, q).start(), k)[1], 0)
+        rin[...] = jnp.zeros_like(rin)
+
+    @pl.when(c == nc - 1)
+    def _():
+        lax.fori_loop(0, CHUNKS, lambda q, k: (left(own, q).start(), k)[1], 0)
+        lin[...] = jnp.zeros_like(lin)
+
+    my_col = r // ratio
+
+    def v_copy(group):
+        place = v.at[
+            pl.ds(pl.multiple_of(lax.rem(r, ratio) * part_p, part_p), part_p),
+            pl.ds(pl.multiple_of(c * width, width), width),
+        ]
+        slot = lax.rem(r, ratio) * nc + c
+        return remote(inn.at[group], place, vsend.at[group], vrecv.at[slot], {"row": group, "col": my_col})
+
+    def v_local():
+        place = v.at[
+            pl.ds(pl.multiple_of(lax.rem(r, ratio) * part_p, part_p), part_p),
+            pl.ds(pl.multiple_of(c * width, width), width),
+        ]
+        return pltpu.make_async_copy(inn.at[r], place, vself)
+
+    for shift in range(nr):
+        group = lax.rem(r + shift, nr)
+        if shift == 0:
+            @pl.when(my_col == c)
+            def _():
+                v_local().start()
+
+            @pl.when(my_col != c)
+            def _():
+                v_copy(group).start()
+        else:
+            v_copy(group).start()
+
+    steps = CHUNKS + nc - 2
+
+    def relay(t, carry):
+        q = t - (c - 1)
+
+        @pl.when((c > 0) & (q >= 0) & (q < CHUNKS))
+        def _():
+            right(own, q).wait_recv()
+
+            @pl.when(c < nc - 1)
+            def _():
+                rtx[chunk(q)] = rin[chunk(q)] + own[chunk(q)]
+                right(rtx, q).start()
+
+        p = t - (nc - 2 - c)
+
+        @pl.when((c < nc - 1) & (p >= 0) & (p < CHUNKS))
+        def _():
+            left(own, p).wait_recv()
+
+            @pl.when(c > 0)
+            def _():
+                ltx[chunk(p)] = lin[chunk(p)] + own[chunk(p)]
+                left(ltx, p).start()
+
+        return carry
+
+    turns = spread.stages + 1
+    begin = 0
+    for turn in range(turns):
+        end = 1 + (steps - 1) * (turn + 1) // (turns + 1)
+        lax.fori_loop(begin, end, relay, 0)
+        begin = end
+        spread.advance(turn)
+    lax.fori_loop(begin, steps, relay, 0)
+
+    def total(q, carry):
+        out[chunk(q)] = own[chunk(q)] + (rin[chunk(q)] + lin[chunk(q)])
+        return carry
+
+    lax.fori_loop(0, CHUNKS, total, 0)
+
+    @pl.when(c < nc - 1)
+    def _():
+        lax.fori_loop(0, CHUNKS, lambda q, k: (right(own, q).wait_send(), k)[1], 0)
+
+    @pl.when(c > 0)
+    def _():
+        lax.fori_loop(0, CHUNKS, lambda q, k: (left(own, q).wait_send(), k)[1], 0)
+
+    spread.finish()
+    for shift in range(nr):
+        group = lax.rem(r + shift, nr)
+        if shift == 0:
+            @pl.when(my_col == c)
+            def _():
+                v_local().wait()
+
+            @pl.when(my_col != c)
+            def _():
+                v_copy(group).wait_send()
+        else:
+            v_copy(group).wait_send()
+    for a in range(ratio):
+        for b in range(nc):
+            @pl.when((r != ratio * c + a) | (c != b))
+            def _():
+                place = v.at[pl.ds(a * part_p, part_p), pl.ds(b * width, width)]
+                remote(
+                    inn.at[0], place, vsend.at[0], vrecv.at[a * nc + b], {"row": r, "col": c}
+                ).wait_recv()
+
+
+def gather(nr, nc, own, rowp, inn):
+    rows, width = own.shape
+    vmem = pl.BlockSpec(memory_space=pltpu.VMEM)
+    ratio = nr // nc
+    big = pltpu.VMEM((rows, width), jnp.float32)
+    sems = pltpu.SemaphoreType.DMA((CHUNKS,))
+    return pl.pallas_call(
+        functools.partial(gather_kernel, nr, nc),
+        out_shape=(
+            jax.ShapeDtypeStruct(own.shape, own.dtype),
+            jax.ShapeDtypeStruct(rowp.shape, rowp.dtype),
+            jax.ShapeDtypeStruct((ratio * inn.shape[1], nc * inn.shape[2]), inn.dtype),
+        ),
+        in_specs=[vmem] * 3,
+        out_specs=(vmem,) * 3,
+        scratch_shapes=[big] * 4 + [sems] * 4
+        + spread_scratch(nr, rowp.shape, rowp.dtype)
+        + [
+            pltpu.SemaphoreType.DMA((nr,)),
+            pltpu.SemaphoreType.DMA((ratio * nc,)),
+            pltpu.SemaphoreType.DMA,
+        ],
+        compiler_params=pltpu.CompilerParams(has_side_effects=True),
+    )(own, rowp, inn)
+
+
+def spread_kernel(nr, in_ref, out_ref, core, hop, send, recv):
+    spread = RowSpread(nr, in_ref, out_ref, core, hop, send, recv)
+    spread.start()
+    for turn in range(spread.stages + 1):
+        spread.advance(turn)
+    spread.finish()
+
+
+def spread_rows(nr, value):
+    vmem = pl.BlockSpec(memory_space=pltpu.VMEM)
+    return pl.pallas_call(
+        functools.partial(spread_kernel, nr),
+        out_shape=jax.ShapeDtypeStruct(value.shape, value.dtype),
+        in_specs=[vmem],
+        out_specs=vmem,
+        scratch_shapes=spread_scratch(nr, value.shape, value.dtype),
+        compiler_params=pltpu.CompilerParams(has_side_effects=True),
+    )(value)
+
+
 def locate(block_owner, target):
     positions = jnp.arange(block_owner.shape[0], dtype=jnp.int32)
     return jnp.sum(jnp.where(block_owner == target, positions, 0))
@@ -256,6 +527,7 @@
     column_blocks = local_cols // B
     r_here = lax.axis_index("row")
     c_here = lax.axis_index("col")
+    nr, nc = lax.axis_size("row"), lax.axis_size("col")
     g = panel_index[0]
     slots = [locate(block_owner, g + t) for t in range(PANELS)]
     rroot = [s // row_blocks for s in slots]
@@ -263,11 +535,6 @@
     rstart = [s % row_blocks * B for s in slots]
     cstart = [s % column_blocks * B for s in slots]
 
-    def block(t, u):
-        tile = lax.dynamic_slice(covariance, (rstart[t], cstart[u]), (B, B))
-        return jnp.where((r_here == rroot[t]) & (c_here == croot[u]), tile, 0.0)
-
-    blocks = lax.psum(jnp.stack([block(0, 0), block(1, 0), block(1, 1)]), ("row", "col"))
     cols = jnp.concatenate(
         [
             jnp.where(c_here == croot[t], lax.dynamic_slice_in_dim(covariance, cstart[t], B, 1), 0.0)
@@ -275,7 +542,6 @@
         ],
         axis=1,
     )
-    cols = lax.psum(cols, "col")
     rowpanel = jnp.concatenate(
         [
             jnp.where(r_here == rroot[t], lax.dynamic_slice_in_dim(covariance, rstart[t], B, 0), 0.0)
@@ -283,24 +549,16 @@
         ],
         axis=0,
     )
-    rowpanel = lax.psum(rowpanel.astype(jnp.bfloat16), "row")
-
-    relaid = lax.all_to_all(
-        lax.all_to_all(innovations, "row", split_axis=1, concat_axis=0, tiled=True),
-        "col",
-        split_axis=0,
-        concat_axis=2,
-        tiled=True,
-    )
-    v = relaid.reshape(relaid.shape[0], local_rows)
-    vs = jnp.concatenate(
-        [
-            jnp.where(r_here == rroot[t], lax.dynamic_slice_in_dim(v, rstart[t], B, 1), 0.0)
-            for t in range(PANELS)
-        ],
-        axis=1,
-    )
-    vs = lax.psum(vs, "row")
+    cols, rowpanel, v = gather(nr, nc, cols, rowpanel.astype(jnp.bfloat16), innovations.transpose(1, 0, 2))
+
+    def pick(value, t, axis):
+        tile = lax.dynamic_slice_in_dim(value, rstart[t], B, axis)
+        return jnp.where(r_here == rroot[t], tile, 0.0)
+
+    parts = [pick(cols[:, :B], 0, 0), pick(cols[:, :B], 1, 0), pick(cols[:, B:], 1, 0), pick(v, 0, 1), pick(v, 1, 1)]
+    everyone = spread_rows(nr, jnp.concatenate(parts, axis=0))
+    blocks = everyone[: 3 * B].reshape(3, B, B)
+    vs = everyone[3 * B :].reshape(PANELS, -1, B)
 
     upper, z, x = factor_pair(blocks)
     tri = jnp.tril(jnp.ones((B, B), jnp.bool_))
@@ -310,9 +568,9 @@
     ro = lax.dynamic_slice_in_dim(block_owner, r_here * row_blocks, row_blocks)
     co = lax.dynamic_slice_in_dim(block_owner, c_here * column_blocks, column_blocks)
     full, half = solve_rows(ro, at, cols, z, x)
-    w0 = dot3(vs[:, :B], z[0], LAST)
+    w0 = dot(vs[0], z[0], LAST, HIGHEST)
     w0h = w0.astype(jnp.bfloat16)
-    w1 = dot3(vs[:, B:] - dot(w0h, x, LAST), z[1], LAST)
+    w1 = dot(vs[1] - dot(w0h, x, LAST), z[1], LAST, HIGHEST)
     w1h = w1.astype(jnp.bfloat16)
     owner_lane = jnp.repeat(ro, B)[None, :]
     wide0 = jnp.tile(w0, (1, row_blocks))

time: 404 us -> 205 us (0.51)
  waiting for transfers between devices: 287 us -> 0 us
  Pallas kernels: 50.2 us -> 171 us
  blocking collectives: 14.7 us -> 0 us
  between operations: 19.8 us -> 6.77 us
  starting transfers between devices: 5 us -> 0 us
  local copies, waits for them, and re-layouts: 5.49 us -> 9.92 us
    psum x4 -> x0, waiting for transfers between devices: 284 us -> none  [the longest x1 116 us: per_device(): lax.psum(jnp.stack([block(0, 0), block(1, 0), block(1, 1)]), ('row', 'col'))]
    pallas_call x0 -> x2, Pallas kernels: none -> 121 us  [the longest x1 94.4 us: gather(): pl.pallas_call(functools.partial(gather_kernel, nr, nc), out_shape=(jax.S...]
    all_to_all x1 -> x0, blocking collectives: 14.7 us -> none  [per_device(): lax.all_to_all(innovations, 'row', split_axis=1, concat_axis=0, tiled=True)]
    all_to_all x1 -> x0, starting transfers between devices: 4.87 us -> none  [per_device(): lax.all_to_all(lax.all_to_all(innovations, 'row', split_axis=1, concat_ax...]
  transfers between devices with their start and end apart: 5 -> 0, of which waited for: 5 -> 0; matrix products, arithmetic and copies ran while one was open for 6% -> 0% of each run, Pallas kernels for 7% -> 0%
where the time goes in v2:
time: 205 us
  Pallas kernels  171 us (83%)
  other arithmetic  11.7 us (6%)
  local copies, waits for them, and re-layouts  9.92 us (5%)
  between operations  6.77 us (3%)
  matrix products  5.42 us (3%)
    pallas_call x1, Pallas kernels, gather(): pl.pallas_call(functools.partial(gather_kernel, nr, nc), out_shape=(jax.S...  94.4 us
    pallas_call x1, Pallas kernels, spread_rows(): pl.pallas_call(functools.partial(spread_kernel, nr), out_shape=jax.ShapeD...  26.3 us
    pallas_call x1, Pallas kernels, factor_pair(): pl.pallas_call(factor_kernel, out_shape=(jax.ShapeDtypeStruct((PANELS, B,...  23.1 us
    pallas_call x1, Pallas kernels, update(): pl.pallas_call(functools.partial(update_kernel, rb=rows // B), grid_spec=...  20.6 us
    pallas_call x1, Pallas kernels, solve_rows(): pl.pallas_call(functools.partial(panel_kernel, blocks=rows // B), grid_sp...  6.43 us
    dot_general x4, matrix products, dot(): lax.dot_general(a, b, dims, precision=precision, preferred_element_type=j...  5.42 us

profile of v2, /device:TPU:0, one launch (start us, length us, event | category | flops | bytes accessed | tf_op | source)
XLA Modules:
  0.0 204.6 jit_solution(12479910432981755241)
XLA Ops:
  1.3 1.3 dynamic_slice.34.co_ref
  2.6 0.7 broadcast_compare_fusion.1
  3.3 0.0 copy-start.4
  3.3 0.1 broadcast_in_dim.66
  3.4 0.1 broadcast_in_dim.68
  3.5 1.3 fusion.8
  10.1 2.0 copy.11
  12.1 1.7 dynamic-slice_select_fusion.1
  13.8 0.0 copy-done.4
  13.8 1.6 pad_maximum_fusion.own
  15.5 2.7 %select_convert_fusion.1 = (bf16[256,2048]{1,0:T(8,128)(2,1)S(1)}, bf16[256,2048]{1,0:T(8,128)(2,1)S(1)}) fusion(f32[1024,2048]{1,0:T(8,128)} %w_ref.1, s32[]{:T(128)S(6)} %select_n.155, pred[]{:T(512)S(6)} %eq.70, s32[]{:T(128)S(6)} %select_n.160, pred[]{:T(512)S(6)} %eq.71), kind=kLoop, calls=%fused_computation.3 | loop fusion | flops 1048576 | bytes 4194314 | tf_op jit(solution)/shard_map/convert
  18.2 1.6 pad_maximum_fusion.1.rowp
  19.8 94.4 %shard_map.59 = (f32[1024,512]{1,0:T(8,128)}, bf16[512,2048]{1,0:T(8,128)(2,1)}, f32[128,1024]{1,0:T(8,128)}) custom-call(f32[1024,512]{1,0:T(8,128)} %pad_maximum_fusion.own, bf16[512,2048]{1,0:T(8,128)(2,1)} %pad_maximum_fusion.1.rowp, f32[8,64,256]{2,1,0:T(8,128)} %bitcast.29), custom_call_target="tpu_custom_call" | custom-call | tf_op jit(solution)/shard_map/pallas_call | solution.py:479
  114.1 0.0 copy-start.3
  114.1 1.7 fusion.11
  116.0 0.0 copy-done.3
  116.0 0.0 copy-start.1
  116.1 1.0 copy-done.1
  117.0 26.3 %shard_map.60 = f32[1024,256]{1,0:T(8,128)} custom-call(f32[1024,256]{1,0:T(8,128)} %copy-done.1), custom_call_target="tpu_custom_call" | custom-call | tf_op jit(solution)/shard_map/pallas_call | solution.py:509
  143.3 2.1 %slice.29 = f32[768,256]{1,0:T(8,128)} slice(f32[1024,256]{1,0:T(8,128)} %shard_map.60), slice={[0:768], [0:256]} | slice | bytes 1572864 | tf_op jit(solution)/shard_map/slice | solution.py:560
  145.4 23.1 %shard_map.61 = (f32[2,256,256]{2,1,0:T(8,128)}, f32[2,256,256]{2,1,0:T(8,128)}, bf16[256,256]{1,0:T(8,128)(2,1)}) custom-call(f32[3,256,256]{2,1,0:T(8,128)} %bitcast.28), custom_call_target="tpu_custom_call" | custom-call | flops 100000000 | bytes 2000000 | tf_op jit(solution)/shard_map/pallas_call | solution.py:134
  168.5 0.0 copy-start.2
  168.5 1.3 copy.7
  169.8 2.0 bitcast_select_fusion
  171.7 0.0 copy-start
  171.7 1.4 fusion.12
  173.2 0.0 copy-done.2
  173.2 1.1 convolution_subtract_fusion.1
  174.3 0.4 fusion.13
  174.7 0.1 tile.20
  174.8 0.1 copy.9
  174.9 0.1 tile.8
  175.0 0.1 copy.8
  175.1 0.0 copy-done
  175.1 6.4 %shard_map.62 = (f32[1024,512]{1,0:T(8,128)}, bf16[1024,512]{1,0:T(8,128)(2,1)}) custom-call(s32[4]{0:T(128)} %copy-done.4, s32[1]{0:T(128)} %copy.16.at_ref, f32[1024,512]{1,0:T(8,128)} %get-tuple-element.11.cols_ref, f32[2,256,256]{2,1,0:T(8,128)} %copy-done, bf16[256,256]{1,0:T(8,128)(2,1)} %get-tuple-element.14.x_ref), custom_call_target="tpu_custom_call" | custom-call | tf_op jit(solution)/shard_map/pallas_call | solution.py:168
  181.5 2.5 %fusion.1 = f32[128,1024]{1,0:T(8,128)} fusion(f32[128,1024]{1,0:T(8,128)S(1)} %bitcast.33, f32[128,1024]{1,0:T(8,128)S(1)} %bitcast.32, f32[128,1024]{1,0:T(8,128)S(1)} %copy-done.3, bf16[1024,512]{1,0:T(8,128)(2,1)} %get-tuple-element.15.half_ref, pred[1024]{0:T(1024)(128)(4,1)S(1)} %eq.77, pred[1024]{0:T(1024)(128)(4,1)S(1)} %eq.74, ...), kind=kOutput, calls=%fused_computation.6 | convolution fusion | flops 134873088 | bytes 3278848 | tf_op jit(solution)/shard_map/dot_general | solution.py:24
  184.0 20.6 %shard_map.63 = f32[1024,2048]{1,0:T(8,128)} custom-call(s32[4]{0:T(128)} %copy-done.4, s32[8]{0:T(128)} %dynamic_slice.34.co_ref, s32[1]{0:T(128)} %copy.16.at_ref, f32[1024,2048]{1,0:T(8,128)} %w_ref.1, bf16[512,2048]{1,0:T(8,128)(2,1)} %get-tuple-element.10.r_ref, f32[2,256,256]{2,1,0:T(8,128)} %copy-done, bf16[256,256]{1,0:T(8,128)(2,1)} %get-tuple-element.14.x_ref, ...), custom_call_target="tpu_custom_call" | custom-call | tf_op jit(solution)/shard_map/pallas_call | solution.py:228
  (9 shorter events, 0.2 us)
Async XLA Ops:
  3.3 10.5 %copy-start.4 = (s32[4]{0:T(128)}, s32[4]{0:T(128)S(1)}, u32[]{:S(2)}) copy-start(s32[4]{0:T(128)S(1)} %get-tuple-element.21.owner_ref.ro_ref) | copy-start | bytes 52
  114.1 1.9 copy-start.3
  116.0 1.0 copy-start.1
  168.5 4.7 %copy-start.2 = (bf16[256,256]{1,0:T(8,128)(2,1)S(1)}, bf16[256,256]{1,0:T(8,128)(2,1)}, u32[]{:S(2)}) copy-start(bf16[256,256]{1,0:T(8,128)(2,1)} %get-tuple-element.14.x_ref) | copy-start | bytes 393220
  171.7 3.4 %copy-start = (f32[2,256,256]{2,1,0:T(8,128)}, f32[2,256,256]{2,1,0:T(8,128)S(1)}, u32[]{:S(2)}) copy-start(f32[2,256,256]{2,1,0:T(8,128)S(1)} %get-tuple-element.29.z_ref) | copy-start | bytes 1572868

commit v3 on v2

--- a/solution.py
+++ b/solution.py
@@ -85,10 +85,10 @@
                 rows[g][t] = v
 
 
-def factor_kernel(d_ref, u_ref, z_ref, x_ref, a_ref, s_ref, p_ref):
+def factor_kernel(d_ref, f_ref, z_ref, x_ref, a_ref, s_ref, p_ref, u_ref):
     row_i = lax.broadcasted_iota(jnp.int32, (B, B), 0)
     col_i = lax.broadcasted_iota(jnp.int32, (B, B), 1)
-    a_ref[...] = d_ref[0]
+    a_ref[...] = d_ref[:B]
 
     def panel(turn, carry):
         s_ref[:, :B] = a_ref[...]
@@ -97,7 +97,7 @@
         def step(k, carry):
             factor_panel(s_ref, p_ref)
             start = pl.multiple_of(k * SUB, SUB)
-            u_ref[turn, pl.ds(start, SUB), :] = pltpu.roll(p_ref[:, :B], start, 1)
+            u_ref[pl.ds(start, SUB), :] = pltpu.roll(p_ref[:, :B], start, 1)
             z_ref[turn, pl.ds(start, SUB), :] = p_ref[:, B:]
             left = p_ref[:, :B]
             rolled = pltpu.roll(left, B - SUB, 1)
@@ -117,13 +117,15 @@
 
         lax.fori_loop(0, B // SUB, step, 0)
 
+        z_ref[turn] = jnp.where(row_i >= col_i, z_ref[turn], 0.0)
+        f_ref[turn] = jnp.where(row_i >= col_i, u_ref[...].T, 0.0)
+
         @pl.when(turn == 0)
         def _():
-            zt = jnp.where(row_i >= col_i, z_ref[0], 0.0)
-            low = dot3(d_ref[1], zt, LAST)
+            low = dot3(d_ref[B : 2 * B], z_ref[0], LAST)
             half = low.astype(jnp.bfloat16)
             x_ref[...] = half
-            a_ref[...] = d_ref[2] - dot(half, half, LAST)
+            a_ref[...] = d_ref[2 * B : 3 * B] - dot(half, half, LAST)
 
         return carry
 
@@ -142,107 +144,144 @@
             pltpu.VMEM((B, B), jnp.float32),
             pltpu.VMEM((B, 2 * B), jnp.float32),
             pltpu.VMEM((SUB, 2 * B), jnp.float32),
+            pltpu.VMEM((B, B), jnp.float32),
         ],
         cost_estimate=pl.CostEstimate(flops=100_000_000, bytes_accessed=2_000_000, transcendentals=0),
     )(blocks)
 
 
-def panel_kernel(owner_ref, at_ref, cols_ref, z_ref, x_ref, out_ref, half_ref, *, blocks):
-    i = pl.program_id(0)
-    own = owner_ref[i]
+def tail_kernel(
+    ro_ref, co_ref, at_ref, w_ref, cols_ref, rowp_ref, f_ref, z_ref, x_ref, vs_ref, v_ref,
+    o_ref, vout_ref, q_ref, full_ref, half_ref, *, rb, cb,
+):
+    j = pl.program_id(0)
     g = at_ref[0]
-    p0 = dot3(cols_ref[:, :B], z_ref[0], LAST)
-    p0 = jnp.where(own > g, p0, 0.0)
-    h0 = p0.astype(jnp.bfloat16)
-    c1 = cols_ref[:, B:] - dot(h0, x_ref[...], LAST)
-    p1 = dot3(c1, z_ref[1], LAST)
-    p1 = jnp.where(own > g + 1, p1, 0.0)
-    out_ref[:, :B] = p0
-    out_ref[:, B:] = p1
-    half_ref[:, :B] = h0
-    half_ref[:, B:] = p1.astype(jnp.bfloat16)
-
-
-def solve_rows(owner, at, cols, z, x):
-    rows = cols.shape[0]
+
+    @pl.when(j == 0)
+    def _():
+        h, n = vs_ref.shape[0] // 2, v_ref.shape[0]
+        x = x_ref[...]
+        for k in range(cb):
+            span = slice(k * B, (k + 1) * B)
+            own = co_ref[k]
+            q0 = dot3(z_ref[0], rowp_ref[:B, span].astype(jnp.float32))
+            q0 = jnp.where(own > g, q0, 0.0).astype(jnp.bfloat16)
+            r1 = rowp_ref[B:, span].astype(jnp.float32) - dot(x, q0)
+            q1 = dot3(z_ref[1], r1)
+            q_ref[:B, span] = q0
+            q_ref[B:, span] = jnp.where(own > g + 1, q1, 0.0).astype(jnp.bfloat16)
+        for i in range(rb):
+            span = slice(i * B, (i + 1) * B)
+            own = ro_ref[i]
+            p0 = dot3(cols_ref[span, :B], z_ref[0], LAST)
+            p0 = jnp.where(own > g, p0, 0.0)
+            h0 = p0.astype(jnp.bfloat16)
+            c1 = cols_ref[span, B:] - dot(h0, x, LAST)
+            p1 = dot3(c1, z_ref[1], LAST)
+            p1 = jnp.where(own > g + 1, p1, 0.0)
+            full_ref[span, :B] = p0
+            full_ref[span, B:] = p1
+            half_ref[span, :B] = h0
+            half_ref[span, B:] = p1.astype(jnp.bfloat16)
+        w0 = dot(vs_ref[:h], z_ref[0], LAST, HIGHEST)
+        w0h = w0.astype(jnp.bfloat16)
+        w1 = dot(vs_ref[h:] - dot(w0h, x, LAST), z_ref[1], LAST, HIGHEST)
+        w1h = w1.astype(jnp.bfloat16)
+        for i in range(rb):
+            span = slice(i * B, (i + 1) * B)
+            own = ro_ref[i]
+            new = v_ref[:, span] - (dot(w0h, half_ref[span, :B], LAST) + dot(w1h, half_ref[span, B:], LAST))
+            new = jnp.where(own == g, w0, new)
+            vout_ref[:, span] = jnp.where(own == g + 1, w1, new)
+
+    cown = co_ref[j]
+    start = pl.multiple_of(j * B, B)
+    o_ref[...] = w_ref[...] - dot(half_ref[...], q_ref[:, pl.ds(start, B)])
+
+    @pl.when(cown > g)
+    def _():
+        for i in range(rb):
+            rown = ro_ref[i]
+
+            @pl.when((rown == g) | ((rown == g + 1) & (cown > g + 1)))
+            def _():
+                o_ref[i * B : (i + 1) * B] = jnp.zeros((B, B), jnp.float32)
+
+    for turn in range(PANELS):
+        @pl.when(cown == g + turn)
+        def _():
+            for i in range(rb):
+                span = slice(i * B, (i + 1) * B)
+                rown = ro_ref[i]
+
+                @pl.when(rown > g + turn)
+                def _():
+                    o_ref[span] = full_ref[span, turn * B : (turn + 1) * B]
+
+                @pl.when(rown == g + turn)
+                def _():
+                    o_ref[span] = f_ref[turn]
+
+
+def tail(ro, co, at, w, cols, rowp, factors, z, x, everyone, v):
+    rows, width = w.shape
+    fixed = lambda rank, *at: (lambda j, a, b, c: tuple(at) if at else (0,) * rank)
+    stripe = lambda j, a, b, c: (0, j)
+    heads = everyone.shape[0] - 3 * B
+    whole = lambda x: pl.BlockSpec(x.shape, fixed(x.ndim))
     return pl.pallas_call(
-        functools.partial(panel_kernel, blocks=rows // B),
+        functools.partial(tail_kernel, rb=rows // B, cb=width // B),
         grid_spec=pltpu.PrefetchScalarGridSpec(
-            num_scalar_prefetch=2,
-            grid=(rows // B,),
+            num_scalar_prefetch=3,
+            grid=(width // B,),
             in_specs=[
-                pl.BlockSpec((B, 2 * B), lambda i, o, a: (i, 0)),
-                pl.BlockSpec((PANELS, B, B), lambda i, o, a: (0, 0, 0)),
-                pl.BlockSpec((B, B), lambda i, o, a: (0, 0)),
+                pl.BlockSpec((rows, B), stripe),
+                whole(cols),
+                whole(rowp),
+                whole(factors),
+                whole(z),
+                whole(x),
+                pl.BlockSpec((heads, B), fixed(2, 3 * B // heads, 0)),
+                whole(v),
+            ],
+            out_specs=[pl.BlockSpec((rows, B), stripe), whole(v)],
+            scratch_shapes=[
+                pltpu.VMEM((2 * B, width), jnp.bfloat16),
+                pltpu.VMEM((rows, 2 * B), jnp.float32),
+                pltpu.VMEM((rows, 2 * B), jnp.bfloat16),
+            ],
+        ),
+        out_shape=(jax.ShapeDtypeStruct(w.shape, w.dtype), jax.ShapeDtypeStruct(v.shape, v.dtype)),
+    )(ro, co, at, w, cols, rowp, factors, z, x, everyone, v)
+
+
+def prep_kernel(at_ref, wc_ref, wr_ref, cols_ref, rowp_ref):
+    t = pl.program_id(0)
+    cols_ref[...] = jnp.where(at_ref[4 + t] > 0, wc_ref[...], 0.0)
+    rowp_ref[...] = jnp.where(at_ref[6 + t] > 0, wr_ref[...], 0.0).astype(jnp.bfloat16)
+
+
+def prep(at, w):
+    rows, width = w.shape
+    return pl.pallas_call(
+        prep_kernel,
+        grid_spec=pltpu.PrefetchScalarGridSpec(
+            num_scalar_prefetch=1,
+            grid=(PANELS,),
+            in_specs=[
+                pl.BlockSpec((rows, B), lambda t, a: (0, a[t])),
+                pl.BlockSpec((B, width), lambda t, a: (a[2 + t], 0)),
             ],
             out_specs=[
-                pl.BlockSpec((B, 2 * B), lambda i, o, a: (i, 0)),
-                pl.BlockSpec((B, 2 * B), lambda i, o, a: (i, 0)),
+                pl.BlockSpec((rows, B), lambda t, a: (0, t)),
+                pl.BlockSpec((B, width), lambda t, a: (t, 0)),
             ],
         ),
         out_shape=(
-            jax.ShapeDtypeStruct((rows, 2 * B), jnp.float32),
-            jax.ShapeDtypeStruct((rows, 2 * B), jnp.bfloat16),
+            jax.ShapeDtypeStruct((rows, PANELS * B), jnp.float32),
+            jax.ShapeDtypeStruct((PANELS * B, width), jnp.bfloat16),
         ),
-    )(owner, at, cols, z, x)
-
-
-def update_kernel(ro_ref, co_ref, at_ref, w_ref, r_ref, z_ref, x_ref, half_ref, full_ref, f_ref, o_ref, *, rb):
-    j = pl.program_id(0)
-    g = at_ref[0]
-    cown = co_ref[j]
-    q0 = dot3(z_ref[0], r_ref[:B].astype(jnp.float32))
-    q0 = jnp.where(cown > g, q0, 0.0).astype(jnp.bfloat16)
-    r1 = r_ref[B:].astype(jnp.float32) - dot(x_ref[...], q0)
-    q1 = dot3(z_ref[1], r1)
-    q1 = jnp.where(cown > g + 1, q1, 0.0).astype(jnp.bfloat16)
-    for i in range(rb):
-        span = slice(i * B, (i + 1) * B)
-        rown = ro_ref[i]
-        new = w_ref[span] - (dot(half_ref[span, :B], q0) + dot(half_ref[span, B:], q1))
-        dead = ((rown == g) & (cown > g)) | ((rown == g + 1) & (cown > g + 1))
-        o_ref[span] = jnp.where(dead, 0.0, new)
-
-        @pl.when((cown == g) & (rown > g))
-        def _():
-            o_ref[span] = full_ref[span, :B]
-
-        @pl.when((cown == g) & (rown == g))
-        def _():
-            o_ref[span] = f_ref[0]
-
-        @pl.when((cown == g + 1) & (rown > g + 1))
-        def _():
-            o_ref[span] = full_ref[span, B:]
-
-        @pl.when((cown == g + 1) & (rown == g + 1))
-        def _():
-            o_ref[span] = f_ref[1]
-
-
-def update(ro, co, at, w, rowpanel, z, x, half, full, factors):
-    rows, cols = w.shape
-    fixed2 = lambda j, a, b, c: (0, 0)
-    fixed3 = lambda j, a, b, c: (0, 0, 0)
-    stripe = lambda j, a, b, c: (0, j)
-    return pl.pallas_call(
-        functools.partial(update_kernel, rb=rows // B),
-        grid_spec=pltpu.PrefetchScalarGridSpec(
-            num_scalar_prefetch=3,
-            grid=(cols // B,),
-            in_specs=[
-                pl.BlockSpec((rows, B), stripe),
-                pl.BlockSpec((2 * B, B), stripe),
-                pl.BlockSpec((PANELS, B, B), fixed3),
-                pl.BlockSpec((B, B), fixed2),
-                pl.BlockSpec((rows, 2 * B), fixed2),
-                pl.BlockSpec((rows, 2 * B), fixed2),
-                pl.BlockSpec((PANELS, B, B), fixed3),
-            ],
-            out_specs=pl.BlockSpec((rows, B), stripe),
-        ),
-        out_shape=jax.ShapeDtypeStruct((rows, cols), jnp.float32),
-    )(ro, co, at, w, rowpanel, z, x, half, full, factors)
+    )(at, w, w)
 
 
 MESH = pl.DeviceIdType.MESH
@@ -533,23 +572,14 @@
     rroot = [s // row_blocks for s in slots]
     croot = [s // column_blocks for s in slots]
     rstart = [s % row_blocks * B for s in slots]
-    cstart = [s % column_blocks * B for s in slots]
-
-    cols = jnp.concatenate(
-        [
-            jnp.where(c_here == croot[t], lax.dynamic_slice_in_dim(covariance, cstart[t], B, 1), 0.0)
-            for t in range(PANELS)
-        ],
-        axis=1,
-    )
-    rowpanel = jnp.concatenate(
-        [
-            jnp.where(r_here == rroot[t], lax.dynamic_slice_in_dim(covariance, rstart[t], B, 0), 0.0)
-            for t in range(PANELS)
-        ],
-        axis=0,
-    )
-    cols, rowpanel, v = gather(nr, nc, cols, rowpanel.astype(jnp.bfloat16), innovations.transpose(1, 0, 2))
+    places = jnp.stack(
+        [s % column_blocks for s in slots]
+        + [s % row_blocks for s in slots]
+        + [(c_here == c).astype(jnp.int32) for c in croot]
+        + [(r_here == r).astype(jnp.int32) for r in rroot]
+    ).astype(jnp.int32)
+    cols, rowpanel = prep(places, covariance)
+    cols, rowpanel, v = gather(nr, nc, cols, rowpanel, innovations.transpose(1, 0, 2))
 
     def pick(value, t, axis):
         tile = lax.dynamic_slice_in_dim(value, rstart[t], B, axis)
@@ -557,29 +587,10 @@
 
     parts = [pick(cols[:, :B], 0, 0), pick(cols[:, :B], 1, 0), pick(cols[:, B:], 1, 0), pick(v, 0, 1), pick(v, 1, 1)]
     everyone = spread_rows(nr, jnp.concatenate(parts, axis=0))
-    blocks = everyone[: 3 * B].reshape(3, B, B)
-    vs = everyone[3 * B :].reshape(PANELS, -1, B)
-
-    upper, z, x = factor_pair(blocks)
-    tri = jnp.tril(jnp.ones((B, B), jnp.bool_))
-    factors = jnp.where(tri, upper.transpose(0, 2, 1), 0.0)
-    z = jnp.where(tri, z, 0.0)
-    at = panel_index
+    factors, z, x = factor_pair(everyone)
     ro = lax.dynamic_slice_in_dim(block_owner, r_here * row_blocks, row_blocks)
     co = lax.dynamic_slice_in_dim(block_owner, c_here * column_blocks, column_blocks)
-    full, half = solve_rows(ro, at, cols, z, x)
-    w0 = dot(vs[0], z[0], LAST, HIGHEST)
-    w0h = w0.astype(jnp.bfloat16)
-    w1 = dot(vs[1] - dot(w0h, x, LAST), z[1], LAST, HIGHEST)
-    w1h = w1.astype(jnp.bfloat16)
-    owner_lane = jnp.repeat(ro, B)[None, :]
-    wide0 = jnp.tile(w0, (1, row_blocks))
-    wide1 = jnp.tile(w1, (1, row_blocks))
-    v = v - dot(jnp.concatenate([w0h, w1h], axis=1), half, LAST)
-    v = jnp.where(owner_lane == g, wide0, v)
-    v = jnp.where(owner_lane == g + 1, wide1, v)
-    matrix = update(ro, co, at, covariance, rowpanel, z, x, half, full, factors)
-    return (matrix, v)
+    return tail(ro, co, panel_index, covariance, cols, rowpanel, factors, z, x, everyone, v)
 
 
 def solution(mesh):

time: 205 us -> 185 us (0.902)
  other arithmetic: 11.7 us -> 1.42 us
  matrix products: 5.42 us -> 0 us
  Pallas kernels: 171 us -> 168 us
    dot_general x4 -> x0, matrix products: 5.42 us -> none  [dot(): lax.dot_general(a, b, dims, precision=precision, preferred_element_type=j...]
    select_n x2 -> x0, other arithmetic: 3.64 us -> none  [the longest x1 1.95 us: per_device(): factors = jnp.where(tri, upper.transpose(0, 2, 1), 0.0)]
    concatenate x2 -> x0, other arithmetic: 3.22 us -> none  [the longest x1 1.64 us: per_device(): jnp.concatenate([jnp.where(c_here == croot[t], lax.dynamic_slice_in_dim(c...]
    another operation x1 -> x0, other arithmetic: 2.69 us -> none
    pallas_call x2, Pallas kernels: 27 us -> 24.3 us  [the longest x1 19.3 us: tail(): pl.pallas_call(functools.partial(tail_kernel, rb=rows // B, cb=width // B...]
    slice x1 -> x0, local copies, waits for them, and re-layouts: 2.06 us -> none  [per_device(): blocks = everyone[:3 * B].reshape(3, B, B)]
where the time goes in v3:
time: 185 us; the launch traced here: 184 us
  Pallas kernels  168 us (91%)
  local copies, waits for them, and re-layouts  7.94 us (4%)
  between operations  6.65 us (4%)
    pallas_call x1, Pallas kernels, gather(): pl.pallas_call(functools.partial(gather_kernel, nr, nc), out_shape=(jax.S...  94.4 us
    pallas_call x1, Pallas kernels, spread_rows(): pl.pallas_call(functools.partial(spread_kernel, nr), out_shape=jax.ShapeD...  26.3 us
    pallas_call x1, Pallas kernels, factor_pair(): pl.pallas_call(factor_kernel, out_shape=(jax.ShapeDtypeStruct((PANELS, B,...  23.5 us
    pallas_call x1, Pallas kernels, tail(): pl.pallas_call(functools.partial(tail_kernel, rb=rows // B, cb=width // B...  19.3 us
    pallas_call x1, Pallas kernels, prep(): pl.pallas_call(prep_kernel, grid_spec=pltpu.PrefetchScalarGridSpec(num_sc...  4.99 us

profile of v3, /device:TPU:0, one launch (start us, length us, event | category | flops | bytes accessed | tf_op | source)
XLA Modules:
  0.0 184.4 jit_solution(5912984991636216775)
XLA Ops:
  1.3 1.3 dynamic_slice.21.ro_ref
  2.5 1.3 dynamic_slice.22.co_ref
  3.8 1.3 fusion.1
  10.4 0.7 stack.51.at_ref
  11.1 2.0 %copy.8 = f32[64,8,256]{2,0,1:T(8,128)} copy(f32[64,8,256]{2,1,0:T(8,128)} %param.5) | data formatting | bytes 1048576 | tf_op args[1]
  13.1 5.0 %shard_map.59 = (f32[1024,512]{1,0:T(8,128)}, bf16[512,2048]{1,0:T(8,128)(2,1)}) custom-call(s32[8]{0:T(128)} %stack.51.at_ref, f32[1024,2048]{1,0:T(8,128)} %w_ref.1, f32[1024,2048]{1,0:T(8,128)} %w_ref.1), custom_call_target="tpu_custom_call" | custom-call | tf_op jit(solution)/shard_map/pallas_call | solution.py:266
  18.1 94.4 %shard_map.60 = (f32[1024,512]{1,0:T(8,128)}, bf16[512,2048]{1,0:T(8,128)(2,1)}, f32[128,1024]{1,0:T(8,128)}) custom-call(f32[1024,512]{1,0:T(8,128)} %get-tuple-element.10.own, bf16[512,2048]{1,0:T(8,128)(2,1)} %get-tuple-element.11.rowp, f32[8,64,256]{2,1,0:T(8,128)} %bitcast.14), custom_call_target="tpu_custom_call" | custom-call | tf_op jit(solution)/shard_map/pallas_call | solution.py:518
  112.4 0.0 copy-start.1
  112.5 1.7 fusion.2
  114.3 0.0 copy-done.1
  114.4 0.0 copy-start
  114.4 1.0 copy-done
  115.3 26.3 %shard_map.61.d_ref.vs_ref = f32[1024,256]{1,0:T(8,128)} custom-call(f32[1024,256]{1,0:T(8,128)} %copy-done), custom_call_target="tpu_custom_call" | custom-call | tf_op jit(solution)/shard_map/pallas_call | solution.py:548
  141.6 23.5 %shard_map.62 = (f32[2,256,256]{2,1,0:T(8,128)}, f32[2,256,256]{2,1,0:T(8,128)}, bf16[256,256]{1,0:T(8,128)(2,1)}) custom-call(f32[1024,256]{1,0:T(8,128)} %shard_map.61.d_ref.vs_ref), custom_call_target="tpu_custom_call" | custom-call | flops 100000000 | bytes 2000000 | tf_op jit(solution)/shard_map/pallas_call | solution.py:136
  165.1 19.3 %shard_map.63 = (f32[1024,2048]{1,0:T(8,128)}, f32[128,1024]{1,0:T(8,128)}) custom-call(s32[4]{0:T(128)} %dynamic_slice.21.ro_ref, s32[8]{0:T(128)} %dynamic_slice.22.co_ref, s32[1]{0:T(128)} %copy.13.at_ref, f32[1024,2048]{1,0:T(8,128)} %w_ref.1, f32[1024,512]{1,0:T(8,128)} %get-tuple-element.12.cols_ref, bf16[512,2048]{1,0:T(8,128)(2,1)} %get-tuple-element.13.rowp_ref, ...), custom_call_target="tpu_custom_call" | custom-call | tf_op jit(solution)/shard_map/pallas_call | solution.py:232
  (5 shorter events, 0.1 us)
Async XLA Ops:
  112.4 1.9 %copy-start.1 = (f32[128,1024]{1,0:T(8,128)S(1)}, f32[128,1024]{1,0:T(8,128)}, u32[]{:S(2)}) copy-start(f32[128,1024]{1,0:T(8,128)} %get-tuple-element.14.v_ref) | copy-start | bytes 1572868
  114.4 1.0 copy-start

commit v4 on v3

--- a/solution.py
+++ b/solution.py
@@ -151,7 +151,7 @@
 
 
 def tail_kernel(
-    ro_ref, co_ref, at_ref, w_ref, cols_ref, rowp_ref, f_ref, z_ref, x_ref, vs_ref, v_ref,
+    own_ref, at_ref, w_ref, cols_ref, rowp_ref, f_ref, z_ref, x_ref, vs_ref, v_ref,
     o_ref, vout_ref, q_ref, full_ref, half_ref, *, rb, cb,
 ):
     j = pl.program_id(0)
@@ -163,7 +163,7 @@
         x = x_ref[...]
         for k in range(cb):
             span = slice(k * B, (k + 1) * B)
-            own = co_ref[k]
+            own = own_ref[at_ref[2] + k]
             q0 = dot3(z_ref[0], rowp_ref[:B, span].astype(jnp.float32))
             q0 = jnp.where(own > g, q0, 0.0).astype(jnp.bfloat16)
             r1 = rowp_ref[B:, span].astype(jnp.float32) - dot(x, q0)
@@ -172,7 +172,7 @@
             q_ref[B:, span] = jnp.where(own > g + 1, q1, 0.0).astype(jnp.bfloat16)
         for i in range(rb):
             span = slice(i * B, (i + 1) * B)
-            own = ro_ref[i]
+            own = own_ref[at_ref[1] + i]
             p0 = dot3(cols_ref[span, :B], z_ref[0], LAST)
             p0 = jnp.where(own > g, p0, 0.0)
             h0 = p0.astype(jnp.bfloat16)
@@ -189,19 +189,19 @@
         w1h = w1.astype(jnp.bfloat16)
         for i in range(rb):
             span = slice(i * B, (i + 1) * B)
-            own = ro_ref[i]
+            own = own_ref[at_ref[1] + i]
             new = v_ref[:, span] - (dot(w0h, half_ref[span, :B], LAST) + dot(w1h, half_ref[span, B:], LAST))
             new = jnp.where(own == g, w0, new)
             vout_ref[:, span] = jnp.where(own == g + 1, w1, new)
 
-    cown = co_ref[j]
+    cown = own_ref[at_ref[2] + j]
     start = pl.multiple_of(j * B, B)
     o_ref[...] = w_ref[...] - dot(half_ref[...], q_ref[:, pl.ds(start, B)])
 
     @pl.when(cown > g)
     def _():
         for i in range(rb):
-            rown = ro_ref[i]
+            rown = own_ref[at_ref[1] + i]
 
             @pl.when((rown == g) | ((rown == g + 1) & (cown > g + 1)))
             def _():
@@ -212,7 +212,7 @@
         def _():
             for i in range(rb):
                 span = slice(i * B, (i + 1) * B)
-                rown = ro_ref[i]
+                rown = own_ref[at_ref[1] + i]
 
                 @pl.when(rown > g + turn)
                 def _():
@@ -223,16 +223,16 @@
                     o_ref[span] = f_ref[turn]
 
 
-def tail(ro, co, at, w, cols, rowp, factors, z, x, everyone, v):
+def tail(owner, at, w, cols, rowp, factors, z, x, everyone, v):
     rows, width = w.shape
-    fixed = lambda rank, *at: (lambda j, a, b, c: tuple(at) if at else (0,) * rank)
-    stripe = lambda j, a, b, c: (0, j)
+    fixed = lambda rank, *at: (lambda j, a, b: tuple(at) if at else (0,) * rank)
+    stripe = lambda j, a, b: (0, j)
     heads = everyone.shape[0] - 3 * B
     whole = lambda x: pl.BlockSpec(x.shape, fixed(x.ndim))
     return pl.pallas_call(
         functools.partial(tail_kernel, rb=rows // B, cb=width // B),
         grid_spec=pltpu.PrefetchScalarGridSpec(
-            num_scalar_prefetch=3,
+            num_scalar_prefetch=2,
             grid=(width // B,),
             in_specs=[
                 pl.BlockSpec((rows, B), stripe),
@@ -252,7 +252,7 @@
             ],
         ),
         out_shape=(jax.ShapeDtypeStruct(w.shape, w.dtype), jax.ShapeDtypeStruct(v.shape, v.dtype)),
-    )(ro, co, at, w, cols, rowp, factors, z, x, everyone, v)
+    )(owner, at, w, cols, rowp, factors, z, x, everyone, v)
 
 
 def prep_kernel(at_ref, wc_ref, wr_ref, cols_ref, rowp_ref):
@@ -285,7 +285,8 @@
 
 
 MESH = pl.DeviceIdType.MESH
-CHUNKS = 16
+CHUNKS = 32
+LAG = 5
 
 
 def remote(src, dst, send, recv, where):
@@ -436,10 +437,10 @@
         else:
             v_copy(group).start()
 
-    steps = CHUNKS + nc - 2
+    steps = CHUNKS + LAG * (nc - 2)
 
     def relay(t, carry):
-        q = t - (c - 1)
+        q = t - LAG * (c - 1)
 
         @pl.when((c > 0) & (q >= 0) & (q < CHUNKS))
         def _():
@@ -450,7 +451,7 @@
                 rtx[chunk(q)] = rin[chunk(q)] + own[chunk(q)]
                 right(rtx, q).start()
 
-        p = t - (nc - 2 - c)
+        p = t - LAG * (nc - 2 - c)
 
         @pl.when((c < nc - 1) & (p >= 0) & (p < CHUNKS))
         def _():
@@ -588,9 +589,8 @@
     parts = [pick(cols[:, :B], 0, 0), pick(cols[:, :B], 1, 0), pick(cols[:, B:], 1, 0), pick(v, 0, 1), pick(v, 1, 1)]
     everyone = spread_rows(nr, jnp.concatenate(parts, axis=0))
     factors, z, x = factor_pair(everyone)
-    ro = lax.dynamic_slice_in_dim(block_owner, r_here * row_blocks, row_blocks)
-    co = lax.dynamic_slice_in_dim(block_owner, c_here * column_blocks, column_blocks)
-    return tail(ro, co, panel_index, covariance, cols, rowpanel, factors, z, x, everyone, v)
+    at = jnp.stack([g, r_here * row_blocks, c_here * column_blocks]).astype(jnp.int32)
+    return tail(block_owner, at, covariance, cols, rowpanel, factors, z, x, everyone, v)
 
 
 def solution(mesh):

time: 185 us -> 184 us (level)
  local copies, waits for them, and re-layouts: 7.94 us -> 5.38 us
    dynamic_slice x2 -> x0, local copies, waits for them, and re-layouts: 2.57 us -> none  [the longest x1 1.3 us: per_device(): lax.dynamic_slice_in_dim(block_owner, c_here * column_blocks, column_blocks)]
where the time goes in v4:
time: 184 us; the launch traced here: 183 us
  Pallas kernels  169 us (92%)
  between operations  6.65 us (4%)
  local copies, waits for them, and re-layouts  5.38 us (3%)
  other arithmetic  2.03 us (1%)
    pallas_call x1, Pallas kernels, gather(): pl.pallas_call(functools.partial(gather_kernel, nr, nc), out_shape=(jax.S...  95.1 us
    pallas_call x1, Pallas kernels, spread_rows(): pl.pallas_call(functools.partial(spread_kernel, nr), out_shape=jax.ShapeD...  26.3 us
    pallas_call x1, Pallas kernels, factor_pair(): pl.pallas_call(factor_kernel, out_shape=(jax.ShapeDtypeStruct((PANELS, B,...  23.5 us
    pallas_call x1, Pallas kernels, tail(): pl.pallas_call(functools.partial(tail_kernel, rb=rows // B, cb=width // B...  18.9 us
    pallas_call x1, Pallas kernels, prep(): pl.pallas_call(prep_kernel, grid_spec=pltpu.PrefetchScalarGridSpec(num_sc...  4.99 us

profile of v4, /device:TPU:0, one launch (start us, length us, event | category | flops | bytes accessed | tf_op | source)
XLA Modules:
  0.0 182.9 jit_solution(3336524677775107435)
XLA Ops:
  1.3 0.6 pad_add_fusion.at_ref
  1.9 1.3 fusion.1
  8.5 0.7 stack.63.at_ref
  9.1 2.0 %copy.8 = f32[64,8,256]{2,0,1:T(8,128)} copy(f32[64,8,256]{2,1,0:T(8,128)} %param.5) | data formatting | bytes 1048576 | tf_op args[1]
  11.1 5.0 %shard_map.59 = (f32[1024,512]{1,0:T(8,128)}, bf16[512,2048]{1,0:T(8,128)(2,1)}) custom-call(s32[8]{0:T(128)} %stack.63.at_ref, f32[1024,2048]{1,0:T(8,128)} %w_ref.1, f32[1024,2048]{1,0:T(8,128)} %w_ref.1), custom_call_target="tpu_custom_call" | custom-call | tf_op jit(solution)/shard_map/pallas_call | solution.py:266
  16.1 95.1 %shard_map.60 = (f32[1024,512]{1,0:T(8,128)}, bf16[512,2048]{1,0:T(8,128)(2,1)}, f32[128,1024]{1,0:T(8,128)}) custom-call(f32[1024,512]{1,0:T(8,128)} %get-tuple-element.10.own, bf16[512,2048]{1,0:T(8,128)(2,1)} %get-tuple-element.11.rowp, f32[8,64,256]{2,1,0:T(8,128)} %bitcast.16), custom_call_target="tpu_custom_call" | custom-call | tf_op jit(solution)/shard_map/pallas_call | solution.py:519
  111.3 0.0 copy-start.1
  111.3 1.7 fusion.2
  113.1 0.0 copy-done.1
  113.2 0.0 copy-start
  113.2 1.0 copy-done
  114.2 26.3 %shard_map.61.d_ref.vs_ref = f32[1024,256]{1,0:T(8,128)} custom-call(f32[1024,256]{1,0:T(8,128)} %copy-done), custom_call_target="tpu_custom_call" | custom-call | tf_op jit(solution)/shard_map/pallas_call | solution.py:549
  140.4 23.5 %shard_map.62 = (f32[2,256,256]{2,1,0:T(8,128)}, f32[2,256,256]{2,1,0:T(8,128)}, bf16[256,256]{1,0:T(8,128)(2,1)}) custom-call(f32[1024,256]{1,0:T(8,128)} %shard_map.61.d_ref.vs_ref), custom_call_target="tpu_custom_call" | custom-call | flops 100000000 | bytes 2000000 | tf_op jit(solution)/shard_map/pallas_call | solution.py:136
  163.9 18.9 %shard_map.63 = (f32[1024,2048]{1,0:T(8,128)}, f32[128,1024]{1,0:T(8,128)}) custom-call(s32[32]{0:T(128)} %own_ref.1, s32[3]{0:T(128)} %pad_add_fusion.at_ref, f32[1024,2048]{1,0:T(8,128)} %w_ref.1, f32[1024,512]{1,0:T(8,128)} %get-tuple-element.12.cols_ref, bf16[512,2048]{1,0:T(8,128)(2,1)} %get-tuple-element.13.rowp_ref, ...), custom_call_target="tpu_custom_call" | custom-call | tf_op jit(solution)/shard_map/pallas_call | solution.py:232
  (5 shorter events, 0.1 us)
Async XLA Ops:
  111.3 1.9 %copy-start.1 = (f32[128,1024]{1,0:T(8,128)S(1)}, f32[128,1024]{1,0:T(8,128)}, u32[]{:S(2)}) copy-start(f32[128,1024]{1,0:T(8,128)} %get-tuple-element.14.v_ref) | copy-start | bytes 1572868
  113.2 1.0 copy-start

commit v5 on v4

--- a/solution.py
+++ b/solution.py
@@ -155,7 +155,7 @@
     o_ref, vout_ref, q_ref, full_ref, half_ref, *, rb, cb,
 ):
     j = pl.program_id(0)
-    g = at_ref[0]
+    g = at_ref[8]
 
     @pl.when(j == 0)
     def _():
@@ -163,8 +163,9 @@
         x = x_ref[...]
         for k in range(cb):
             span = slice(k * B, (k + 1) * B)
-            own = own_ref[at_ref[2] + k]
-            q0 = dot3(z_ref[0], rowp_ref[:B, span].astype(jnp.float32))
+            own = own_ref[at_ref[10] + k]
+            zh, zl = split_bf16(z_ref[0])
+            q0 = dot(zh, rowp_ref[:B, span]) + dot(zl, rowp_ref[:B, span])
             q0 = jnp.where(own > g, q0, 0.0).astype(jnp.bfloat16)
             r1 = rowp_ref[B:, span].astype(jnp.float32) - dot(x, q0)
             q1 = dot3(z_ref[1], r1)
@@ -172,7 +173,7 @@
             q_ref[B:, span] = jnp.where(own > g + 1, q1, 0.0).astype(jnp.bfloat16)
         for i in range(rb):
             span = slice(i * B, (i + 1) * B)
-            own = own_ref[at_ref[1] + i]
+            own = own_ref[at_ref[9] + i]
             p0 = dot3(cols_ref[span, :B], z_ref[0], LAST)
             p0 = jnp.where(own > g, p0, 0.0)
             h0 = p0.astype(jnp.bfloat16)
@@ -189,19 +190,19 @@
         w1h = w1.astype(jnp.bfloat16)
         for i in range(rb):
             span = slice(i * B, (i + 1) * B)
-            own = own_ref[at_ref[1] + i]
+            own = own_ref[at_ref[9] + i]
             new = v_ref[:, span] - (dot(w0h, half_ref[span, :B], LAST) + dot(w1h, half_ref[span, B:], LAST))
             new = jnp.where(own == g, w0, new)
             vout_ref[:, span] = jnp.where(own == g + 1, w1, new)
 
-    cown = own_ref[at_ref[2] + j]
+    cown = own_ref[at_ref[10] + j]
     start = pl.multiple_of(j * B, B)
     o_ref[...] = w_ref[...] - dot(half_ref[...], q_ref[:, pl.ds(start, B)])
 
     @pl.when(cown > g)
     def _():
         for i in range(rb):
-            rown = own_ref[at_ref[1] + i]
+            rown = own_ref[at_ref[9] + i]
 
             @pl.when((rown == g) | ((rown == g + 1) & (cown > g + 1)))
             def _():
@@ -212,7 +213,7 @@
         def _():
             for i in range(rb):
                 span = slice(i * B, (i + 1) * B)
-                rown = own_ref[at_ref[1] + i]
+                rown = own_ref[at_ref[9] + i]
 
                 @pl.when(rown > g + turn)
                 def _():
@@ -556,11 +557,6 @@
     )(value)
 
 
-def locate(block_owner, target):
-    positions = jnp.arange(block_owner.shape[0], dtype=jnp.int32)
-    return jnp.sum(jnp.where(block_owner == target, positions, 0))
-
-
 def per_device(covariance, innovations, block_owner, panel_index):
     local_rows, local_cols = covariance.shape
     row_blocks = local_rows // B
@@ -569,28 +565,32 @@
     c_here = lax.axis_index("col")
     nr, nc = lax.axis_size("row"), lax.axis_size("col")
     g = panel_index[0]
-    slots = [locate(block_owner, g + t) for t in range(PANELS)]
-    rroot = [s // row_blocks for s in slots]
-    croot = [s // column_blocks for s in slots]
-    rstart = [s % row_blocks * B for s in slots]
-    places = jnp.stack(
-        [s % column_blocks for s in slots]
-        + [s % row_blocks for s in slots]
-        + [(c_here == c).astype(jnp.int32) for c in croot]
-        + [(r_here == r).astype(jnp.int32) for r in rroot]
-    ).astype(jnp.int32)
+    index = jnp.arange(12, dtype=jnp.int32)
+    positions = jnp.arange(block_owner.shape[0], dtype=jnp.int32)
+    match = block_owner[None, :] == (panel_index[0] + index % PANELS)[:, None]
+    slot = jnp.sum(jnp.where(match, positions[None, :], 0), axis=1)
+    options = [
+        slot % column_blocks,
+        slot % row_blocks,
+        (slot // column_blocks == c_here).astype(jnp.int32),
+        (slot // row_blocks == r_here).astype(jnp.int32),
+        jnp.where(index % PANELS == 0, g, r_here * row_blocks),
+    ]
+    places = c_here * column_blocks
+    for kind, option in reversed(list(enumerate(options))):
+        places = jnp.where(index // PANELS == kind, option, places)
+    places = places.astype(jnp.int32)
     cols, rowpanel = prep(places, covariance)
     cols, rowpanel, v = gather(nr, nc, cols, rowpanel, innovations.transpose(1, 0, 2))
 
     def pick(value, t, axis):
-        tile = lax.dynamic_slice_in_dim(value, rstart[t], B, axis)
-        return jnp.where(r_here == rroot[t], tile, 0.0)
+        tile = lax.dynamic_slice_in_dim(value, places[2 + t] * B, B, axis)
+        return jnp.where(places[6 + t] > 0, tile, 0.0)
 
     parts = [pick(cols[:, :B], 0, 0), pick(cols[:, :B], 1, 0), pick(cols[:, B:], 1, 0), pick(v, 0, 1), pick(v, 1, 1)]
     everyone = spread_rows(nr, jnp.concatenate(parts, axis=0))
     factors, z, x = factor_pair(everyone)
-    at = jnp.stack([g, r_here * row_blocks, c_here * column_blocks]).astype(jnp.int32)
-    return tail(block_owner, at, covariance, cols, rowpanel, factors, z, x, everyone, v)
+    return tail(block_owner, places, covariance, cols, rowpanel, factors, z, x, everyone, v)
 
 
 def solution(mesh):

time: 184 us -> 179 us (0.973)
  between operations: 6.65 us -> 3.96 us
where the time goes in v5:
time: 179 us
  Pallas kernels  169 us (94%)
  local copies, waits for them, and re-layouts  5.33 us (3%)
  between operations  3.96 us (2%)
    pallas_call x1, Pallas kernels, gather(): pl.pallas_call(functools.partial(gather_kernel, nr, nc), out_shape=(jax.S...  95.2 us
    pallas_call x1, Pallas kernels, spread_rows(): pl.pallas_call(functools.partial(spread_kernel, nr), out_shape=jax.ShapeD...  26.3 us
    pallas_call x1, Pallas kernels, factor_pair(): pl.pallas_call(factor_kernel, out_shape=(jax.ShapeDtypeStruct((PANELS, B,...  23.5 us
    pallas_call x1, Pallas kernels, tail(): pl.pallas_call(functools.partial(tail_kernel, rb=rows // B, cb=width // B...  18.7 us
    pallas_call x1, Pallas kernels, prep(): pl.pallas_call(prep_kernel, grid_spec=pltpu.PrefetchScalarGridSpec(num_sc...  4.99 us

profile of v5, /device:TPU:0, one launch (start us, length us, event | category | flops | bytes accessed | tf_op | source)
XLA Modules:
  0.0 178.9 jit_solution(10687983562777738153)
XLA Ops:
  1.3 0.8 select_reduce_fusion
  2.2 0.0 copy-start.2
  2.2 0.6 fusion.1
  5.4 2.0 %copy.9 = f32[64,8,256]{2,0,1:T(8,128)} copy(f32[64,8,256]{2,1,0:T(8,128)} %param.5) | data formatting | bytes 1048576 | tf_op args[1]
  7.4 0.0 copy-done.2
  7.4 5.0 %shard_map.59 = (f32[1024,512]{1,0:T(8,128)}, bf16[512,2048]{1,0:T(8,128)(2,1)}) custom-call(s32[12]{0:T(128)} %copy-done.2, f32[1024,2048]{1,0:T(8,128)} %w_ref.1, f32[1024,2048]{1,0:T(8,128)} %w_ref.1), custom_call_target="tpu_custom_call" | custom-call | tf_op jit(solution)/shard_map/pallas_call | solution.py:267
  12.4 95.2 %shard_map.60 = (f32[1024,512]{1,0:T(8,128)}, bf16[512,2048]{1,0:T(8,128)(2,1)}, f32[128,1024]{1,0:T(8,128)}) custom-call(f32[1024,512]{1,0:T(8,128)} %get-tuple-element.10.own, bf16[512,2048]{1,0:T(8,128)(2,1)} %get-tuple-element.11.rowp, f32[8,64,256]{2,1,0:T(8,128)} %bitcast.10), custom_call_target="tpu_custom_call" | custom-call | tf_op jit(solution)/shard_map/pallas_call | solution.py:520
  107.5 0.0 copy-start.1
  107.5 1.7 fusion
  109.4 0.0 copy-done.1
  109.4 0.0 copy-start
  109.4 1.0 copy-done
  110.4 26.3 %shard_map.61.d_ref.vs_ref = f32[1024,256]{1,0:T(8,128)} custom-call(f32[1024,256]{1,0:T(8,128)} %copy-done), custom_call_target="tpu_custom_call" | custom-call | tf_op jit(solution)/shard_map/pallas_call | solution.py:550
  136.7 23.5 %shard_map.62 = (f32[2,256,256]{2,1,0:T(8,128)}, f32[2,256,256]{2,1,0:T(8,128)}, bf16[256,256]{1,0:T(8,128)(2,1)}) custom-call(f32[1024,256]{1,0:T(8,128)} %shard_map.61.d_ref.vs_ref), custom_call_target="tpu_custom_call" | custom-call | flops 100000000 | bytes 2000000 | tf_op jit(solution)/shard_map/pallas_call | solution.py:136
  160.2 18.7 %shard_map.63 = (f32[1024,2048]{1,0:T(8,128)}, f32[128,1024]{1,0:T(8,128)}) custom-call(s32[32]{0:T(128)} %own_ref.1, s32[12]{0:T(128)} %copy-done.2, f32[1024,2048]{1,0:T(8,128)} %w_ref.1, f32[1024,512]{1,0:T(8,128)} %get-tuple-element.12.cols_ref, bf16[512,2048]{1,0:T(8,128)(2,1)} %get-tuple-element.13.rowp_ref, f32[2,256,256]{2,1,0:T(8,128)} %get-tuple-element.15.f_ref, ...), custom_call_target="tpu_custom_call" | custom-call | tf_op jit(solution)/shard_map/pallas_call | solution.py:233
  (7 shorter events, 0.1 us)
Async XLA Ops:
  2.2 5.2 %copy-start.2 = (s32[12]{0:T(128)}, s32[12]{0:T(128)S(1)}, u32[]{:S(2)}) copy-start(s32[12]{0:T(128)S(1)} %compare_select_fusion.5.at_ref) | copy-start | bytes 148
  107.5 1.9 %copy-start.1 = (f32[128,1024]{1,0:T(8,128)S(1)}, f32[128,1024]{1,0:T(8,128)}, u32[]{:S(2)}) copy-start(f32[128,1024]{1,0:T(8,128)} %get-tuple-element.14.v_ref) | copy-start | bytes 1572868
  109.4 1.0 copy-start
